TPU v7x, 32 devices: a whole 2x2x4 slice. The times are simulated.
32 devices in a mesh: groups: 2 (over y), gz: 4 (over z), xy: 2 (over x), col: 2 (over core).
Axes of the slice: x: 2, y: 2, z: 4, core: 2. Of those that a mesh axis runs over, the one named last changes fastest.
Arguments:
- features: bfloat16 [8, 16, 256, 256], P(('groups', 'gz'), None, ('xy', 'col')), parts along dimension 0, may hold values from -24 to 24
- class_map: int32 [8, 256, 256], P(('groups', 'gz'), ('xy', 'col')), parts along dimension 0, may hold values from 0 to 3
- stiffness: float32 [4], replicated, may hold values from 0.2 to 2
- valid: int32 [8, 4], P('groups'), parts along dimension 0, may hold values 0 or 1
Outputs:
- displacement: float32 [8, 2, 256, 256], P(('groups', 'gz'), None, ('xy', 'col')), parts along dimension 0
- forward_flow: float32 [8, 2, 256, 256], P(('groups', 'gz'), None, ('xy', 'col')), parts along dimension 0
There are 2 independent parts, one for each index of `groups`. A program takes and returns all parts, laid end to end along the dimension named above; an argument that names none is the same for every part. Nothing has to cross between parts.
All inputs are finite; a program needn't handle non-finite values.
Results may differ from a plain program's by a relative error of at most 0.0017.
Values may be sent and summed in bfloat16 or wider, within the bound.
No kernel may reach another device: no remote copies, remote signals or barrier semaphores. Data moves between devices by JAX's collectives and lax.ppermute only.
A program may use at most 64 MiB of HBM per device.

v0:
```python
import math

import jax
import jax.numpy as jnp
from jax import lax
from jax.sharding import PartitionSpec as P

RADIUS = 6
STEPS = 3


score_scale = 0.25
step_size = 0.1
saturation = 2.0


def padded_2(cells, sides, width):
    for axis, dim in sides:
        count = lax.axis_size(axis)
        ends = count - 1
        head = lax.slice_in_dim(cells, 0, width, axis=dim)
        tail = lax.slice_in_dim(cells, cells.shape[dim] - width, cells.shape[dim], axis=dim)
        cells = jnp.concatenate(
            [
                lax.ppermute(tail, axis, [(i, (i + 1) % count) for i in range(ends)]),
                cells,
                lax.ppermute(head, axis, [((i + 1) % count, i) for i in range(ends)]),
            ],
            axis=dim,
        )
    return cells


def passed_along(value, axis, steps):
    count = lax.axis_size(axis)
    initial, last = (max(0, -steps), min(count, count - steps))
    return lax.ppermute(value, axis, [(source, source + steps) for source in range(initial, last)])


def entering(shard, axis, combine, identity):
    length, here = (lax.axis_size(axis), lax.axis_index(axis))
    everything = lax.all_gather(shard, axis)
    start = jnp.broadcast_to(jnp.asarray(identity, shard.dtype), shard.shape)

    def step(k, before):
        reached = k < here
        new = combine(before, everything[k])
        return jnp.where(reached, new, before)

    return lax.fori_loop(0, length, step, start)


def shortened(shard):
    return jax.tree.map(lambda a: a.astype(jnp.bfloat16) if a.dtype == jnp.float32 else a, shard)


def expected(stacked):
    highest = jnp.max(stacked, axis=0)
    weights = jnp.exp(stacked - highest)
    denominator = jnp.sum(weights, axis=0)
    window = 2 * RADIUS + 1
    places = jnp.arange(window * window, dtype=jnp.int32)
    row_shift = (places // window - RADIUS).astype(jnp.float32)
    col_shift = (places % window - RADIUS).astype(jnp.float32)
    flow_row = jnp.sum(weights * row_shift[:, None, None], axis=0) / denominator
    flow_col = jnp.sum(weights * col_shift[:, None, None], axis=0) / denominator
    return jnp.stack([flow_row, flow_col])


def band_scores(center_band, window_band, height, breadth):
    scores = []
    for shift_row in range(2 * RADIUS + 1):
        for shift_col in range(2 * RADIUS + 1):
            scores.append(
                jnp.sum(
                    center_band
                    * window_band[
                        :, shift_row : shift_row + height, shift_col : shift_col + breadth
                    ],
                    axis=0,
                )
            )
    return score_scale * jnp.stack(scores)


def flow_of(center, other):
    channels, height, breadth = center.shape
    band_rows = math.gcd(height, 16)

    def one_band(band_index):
        band_start = band_index * band_rows
        center_band = lax.dynamic_slice_in_dim(center, band_start, band_rows, 1).astype(jnp.float32)
        window_band = lax.dynamic_slice_in_dim(other, band_start, band_rows + 2 * RADIUS, 1).astype(
            jnp.float32
        )
        return expected(band_scores(center_band, window_band, band_rows, breadth))

    results = lax.map(one_band, jnp.arange(height // band_rows, dtype=jnp.int32))
    return jnp.moveaxis(results, 0, 1).reshape(2, height, breadth)


def widen(values_in, margin):
    padding = [(0, 0)] * (values_in.ndim - 1) + [(margin, margin)]
    return jnp.pad(values_in, padding)


def elastic_term(disp_pad, stiff_pad):
    middle = disp_pad[..., 1:-1, 1:-1]
    stiff_mid = stiff_pad[..., 1:-1, 1:-1]
    result = jnp.zeros_like(middle)
    for row_part, col_part in (
        (slice(2, None), slice(1, -1)),
        (slice(0, -2), slice(1, -1)),
        (slice(1, -1), slice(2, None)),
        (slice(1, -1), slice(0, -2)),
    ):
        neighbour_stiff = stiff_pad[..., row_part, col_part]
        result = result + 0.5 * (stiff_mid + neighbour_stiff) * (
            middle - disp_pad[..., row_part, col_part]
        )
    return result


def spring(vector):
    return vector / jnp.sqrt(
        1.0 + jnp.sum(vector * vector, axis=-3, keepdims=True) / (saturation * saturation)
    )


def add_pair(earlier, later):
    return earlier + later


def on_device(features, class_map, stiffness, valid):
    center = features[0]
    height, breadth = (center.shape[1], center.shape[2])
    section = lax.axis_index("gz")
    tile_index = lax.axis_index(("xy", "col"))
    column = lax.dynamic_slice_in_dim(valid, tile_index, 1, 1)[:, 0].astype(jnp.float32)
    link_all = column * jnp.concatenate([column[1:], jnp.zeros((1,), jnp.float32)])
    link_here = lax.dynamic_index_in_dim(link_all, section, 0, keepdims=False)
    link_below = jnp.where(
        section > 0,
        lax.dynamic_index_in_dim(link_all, jnp.maximum(section - 1, 0), 0, keepdims=False),
        0.0,
    )
    padded = widen(padded_2(center, ((("xy", "col"), 1),), RADIUS), RADIUS)
    upper_pad = passed_along(padded, "gz", -1)
    forward = flow_of(center, upper_pad)
    ahead_flow = flow_of(upper_pad[:, RADIUS : RADIUS + height, RADIUS : RADIUS + breadth], padded)
    passed = passed_along(jnp.stack([forward, ahead_flow]), "gz", 1)
    prior_flow = passed[0]
    backward = passed[1]
    excess = link_here * forward - link_below * backward
    before = entering(excess, "gz", add_pair, jnp.zeros_like(excess))
    displace = 0.5 * (before - link_below * backward)
    levels = jnp.arange(stiffness.shape[0], dtype=jnp.int32)
    stiff_field = jnp.sum(
        jnp.where(class_map[0][None] == levels[:, None, None], stiffness[:, None, None], 0.0),
        axis=0,
    )
    stiff_pad = widen(padded_2(stiff_field, ((("xy", "col"), 0),), 1), 1)
    for step_number in range(STEPS):
        disp_pad = widen(padded_2(displace, ((("xy", "col"), 1),), 1), 1)
        elastic = elastic_term(disp_pad, stiff_pad)
        upper_disp = passed_along(shortened(displace), "gz", -1).astype(displace.dtype)
        lower_disp = passed_along(shortened(displace), "gz", 1).astype(displace.dtype)
        pull_up = link_here * spring(upper_disp - displace - forward)
        pull_down = link_below * spring(lower_disp - displace - backward)
        from_below = link_below * spring(displace - lower_disp - prior_flow)
        from_above = link_here * spring(displace - upper_disp - ahead_flow)
        gradient = elastic - pull_up - pull_down + from_below + from_above
        displace = displace - step_size * gradient
    return (displace[None], forward[None])


def solution(mesh):
    placed = (
        P(("groups", "gz"), None, ("xy", "col"), None),
        P(("groups", "gz"), ("xy", "col"), None),
        P(),
        P("groups", None),
    )
    return jax.shard_map(
        on_device,
        mesh=mesh,
        in_specs=placed,
        out_specs=(
            P(("groups", "gz"), None, ("xy", "col"), None),
            P(("groups", "gz"), None, ("xy", "col"), None),
        ),
        check_vma=False,
    )
```

profile of v0, /device:TPU:0, one launch (start us, length us, event | category | flops | bytes accessed | tf_op | source)
XLA Modules:
  0.0 261.7 jit_solution(13074941978492114994)
XLA Ops:
  3.3 3.0 %collective-permute-start = (bf16[16,6,256]{2,0,1:T(8,128)(2,1)S(1)}, bf16[16,6,256]{2,0,1:T(8,128)(2,1)S(1)}, u32[]{:S(2)}, u32[]{:S(2)}) collective-permute-start(bf16[16,6,256]{2,0,1:T(8,128)(2,1)S(1)} %get-tuple-element.723), channel_id=1, source_target_pairs={{0,1},{1,2},{2,3},{4,5},{5,6},{6,7},{8,9},{9,10},{10,11},{12,13},{... | collective-permute-start | bytes 147464 | tf_op jit(solution)/shard_map/ppermute | solution.py:25
  11.6 6.0 %collective-permute-start.6 = (f32[1,256]{1,0:T(1,128)}, f32[1,256]{1,0:T(1,128)}, u32[]{:S(2)}, u32[]{:S(2)}) collective-permute-start(f32[1,256]{1,0:T(1,128)} %get-tuple-element.735), channel_id=1, source_target_pairs={{0,1},{1,2},{2,3},{4,5},{5,6},{6,7},{8,9},{9,10},{10,11},{12,13},{... | collective-permute-start | bytes 3080 | tf_op jit(solution)/shard_map/ppermute | solution.py:25
  19.0 14.4 %collective-permute-done.2 = bf16[16,76,268]{2,0,1:T(8,128)(2,1)S(1)} collective-permute-done((bf16[16,76,268]{2,0,1:T(8,128)(2,1)S(1)}, bf16[16,76,268]{2,0,1:T(8,128)(2,1)S(1)}, u32[]{:S(2)}, u32[]{:S(2)}) %collective-permute-start.2) | collective-permute-done | bytes 651808 | tf_op jit(solution)/shard_map/ppermute | solution.py:37
  33.4 91.1 %while.40 = (s32[]{:T(128)}, f32[4,2,16,256]{3,2,1,0:T(8,128)S(1)}, s32[4]{0:T(128)S(1)}, bf16[16,64,256]{2,1,0:T(8,128)(2,1)}, bf16[16,76,268]{2,0,1:T(8,128)(2...) while((s32[]{:T(128)}, f32[4,2,16,256]{3,2,1,0:T(8,128)S(1)}, ...), condition=%wide.region_174.175_spmd, body=%wide.region_0.174_spmd.sunk | while | flops 28467096 | bytes 62987676 | solution.py:98
  38.3 2.1 fusion.467
  40.6 2.1 fusion.468
  42.9 2.1 fusion.469
  63.4 2.1 fusion.468
  65.7 2.1 fusion.469
  86.2 2.1 fusion.468
  88.5 2.1 fusion.469
  109.0 2.1 fusion.468
  111.3 2.1 fusion.469
  124.8 65.4 %while.41 = (s32[]{:T(128)}, f32[4,2,16,256]{3,2,1,0:T(8,128)S(1)}, s32[4]{0:T(128)S(1)}, bf16[16,64,256]{2,0,1:T(8,128)(2,1)S(1)}, bf16[16,76,268]{2,0,1:T(8,12...) while((s32[]{:T(128)}, f32[4,2,16,256]{3,2,1,0:T(8,128)S(1)}, ...), condition=%wide.region_349.350_spmd, body=%wide.region_175.349_spmd.sunk | while | flops 28467096 | bytes 61152604 | solution.py:98
  190.3 4.4 %collective-permute-start.3 = (f32[2,2,64,256]{3,2,1,0:T(8,128)S(1)}, f32[2,2,64,256]{3,2,1,0:T(8,128)S(1)}, u32[]{:S(2)}, u32[]{:S(2)}) collective-permute-start(f32[2,2,64,256]{3,2,1,0:T(8,128)S(1)} %pad_maximum_fusion), channel_id=1, source_target_pairs={{0,4},{4,8},{8,12},{1,5},{5,9},{9,13},{2,6},{6,10},{10,14},{3,7},{... | collective-permute-start | bytes 786440 | tf_op jit(solution)/shard_map/ppermute | solution.py:37
  197.0 3.7 %collective-permute-done.3 = f32[2,2,64,256]{3,2,1,0:T(8,128)S(1)} collective-permute-done((f32[2,2,64,256]{3,2,1,0:T(8,128)S(1)}, f32[2,2,64,256]{3,2,1,0:T(8,128)S(1)}, u32[]{:S(2)}, u32[]{:S(2)}) %collective-permute-start.3) | collective-permute-done | bytes 262176 | tf_op jit(solution)/shard_map/ppermute | solution.py:37
  201.3 16.1 %all_gather.4 = f32[4,2,64,256]{3,2,1,0:T(8,128)S(1)} all-gather(f32[1,2,64,256]{3,2,1,0:T(8,128)S(1)} %multiply_subtract_fusion), channel_id=1, replica_groups=mesh['groups'=2,'gz'=4,'xy'=2,'col'=2] {'gz'}, dimensions={0}, use_global_device_ids=true | all-gather | bytes 655360 | tf_op jit(solution)/shard_map/all_gather | solution.py:42
  219.0 3.0 %collective-permute-start.7 = (f32[2,1,256]{2,1,0:T(1,128)S(1)}, f32[2,1,256]{2,1,0:T(1,128)S(1)}, u32[]{:S(2)}, u32[]{:S(2)}) collective-permute-start(f32[2,1,256]{2,1,0:T(1,128)S(1)} %get-tuple-element.731), channel_id=1, source_target_pairs={{0,1},{1,2},{2,3},{4,5},{5,6},{6,7},{8,9},{9,10},{10,11},{12,13},{... | collective-permute-start | bytes 6152 | tf_op jit(solution)/shard_map/ppermute | solution.py:25
  224.1 4.5 %collective-permute-start.9 = (bf16[2,64,256]{2,1,0:T(8,128)(2,1)S(1)}, bf16[2,64,256]{2,1,0:T(8,128)(2,1)S(1)}, u32[]{:S(2)}, u32[]{:S(2)}) collective-permute-start(bf16[2,64,256]{2,1,0:T(8,128)(2,1)S(1)} %get-tuple-element.699), channel_id=1, source_target_pairs={{0,4},{4,8},{8,12},{1,5},{5,9},{9,13},{2,6},{6,10},{10,14},{3,7},{... | collective-permute-start | bytes 196616 | tf_op jit(solution)/shard_map/ppermute | solution.py:37
  232.9 3.0 %collective-permute-start.11 = (f32[2,1,256]{2,1,0:T(1,128)S(1)}, f32[2,1,256]{2,1,0:T(1,128)S(1)}, u32[]{:S(2)}, u32[]{:S(2)}) collective-permute-start(f32[2,1,256]{2,1,0:T(1,128)S(1)} %get-tuple-element.729), channel_id=1, source_target_pairs={{0,1},{1,2},{2,3},{4,5},{5,6},{6,7},{8,9},{9,10},{10,11},{12,13},{... | collective-permute-start | bytes 6152 | tf_op jit(solution)/shard_map/ppermute | solution.py:25
  237.3 4.9 %collective-permute-start.13 = (bf16[2,64,256]{2,1,0:T(8,128)(2,1)S(1)}, bf16[2,64,256]{2,1,0:T(8,128)(2,1)S(1)}, u32[]{:S(2)}, u32[]{:S(2)}) collective-permute-start(bf16[2,64,256]{2,1,0:T(8,128)(2,1)S(1)} %get-tuple-element.697), channel_id=1, source_target_pairs={{0,4},{4,8},{8,12},{1,5},{5,9},{9,13},{2,6},{6,10},{10,14},{3,7},{... | collective-permute-start | bytes 196616 | tf_op jit(solution)/shard_map/ppermute | solution.py:37
  246.5 3.0 %collective-permute-start.15 = (f32[2,1,256]{2,1,0:T(1,128)S(1)}, f32[2,1,256]{2,1,0:T(1,128)S(1)}, u32[]{:S(2)}, u32[]{:S(2)}) collective-permute-start(f32[2,1,256]{2,1,0:T(1,128)S(1)} %get-tuple-element.727), channel_id=1, source_target_pairs={{0,1},{1,2},{2,3},{4,5},{5,6},{6,7},{8,9},{9,10},{10,11},{12,13},{... | collective-permute-start | bytes 6152 | tf_op jit(solution)/shard_map/ppermute | solution.py:25
  249.5 4.3 %collective-permute-start.17 = (bf16[2,64,256]{2,1,0:T(8,128)(2,1)S(1)}, bf16[2,64,256]{2,1,0:T(8,128)(2,1)S(1)}, u32[]{:S(2)}, u32[]{:S(2)}) collective-permute-start(bf16[2,64,256]{2,1,0:T(8,128)(2,1)S(1)} %get-tuple-element.695), channel_id=1, source_target_pairs={{0,4},{4,8},{8,12},{1,5},{5,9},{9,13},{2,6},{6,10},{10,14},{3,7},{... | collective-permute-start | bytes 196616 | tf_op jit(solution)/shard_map/ppermute | solution.py:37
  255.7 4.3 %collective-permute-done.16 = bf16[2,64,256]{2,1,0:T(8,128)(2,1)S(1)} collective-permute-done((bf16[2,64,256]{2,1,0:T(8,128)(2,1)S(1)}, bf16[2,64,256]{2,1,0:T(8,128)(2,1)S(1)}, u32[]{:S(2)}, u32[]{:S(2)}) %collective-permute-start.16) | collective-permute-done | bytes 65568 | tf_op jit(solution)/shard_map/ppermute | solution.py:37
  (1588 shorter events, 148.6 us)
Async XLA Ops:
  0.6 8.4 %copy-start.8 = (f32[4]{0:T(128)S(1)}, f32[4]{0:T(128)}, u32[]{:S(2)}) copy-start(f32[4]{0:T(128)} %param.12) | copy-start | bytes 52
  0.7 17.0 %copy-start.5 = (s32[4,4]{1,0:T(4,128)S(1)}, s32[4,4]{1,0:T(4,128)}, u32[]{:S(2)}) copy-start(s32[4,4]{1,0:T(4,128)} %param.13) | copy-start | bytes 196
  2.0 4.3 %collective-permute-start.1 = (bf16[16,6,256]{2,0,1:T(8,128)(2,1)S(1)}, bf16[16,6,256]{2,0,1:T(8,128)(2,1)S(1)}, u32[]{:S(2)}, u32[]{:S(2)}) collective-permute-start(bf16[16,6,256]{2,0,1:T(8,128)(2,1)S(1)} %get-tuple-element.724), channel_id=1, source_target_pairs={{1,0},{2,1},{3,2},{5,4},{6,5},{7,6},{9,8},{10,9},{11,10},{13,12},{... | collective-permute-start | bytes 147464 | tf_op jit(solution)/shard_map/ppermute | solution.py:27
  3.3 3.9 %collective-permute-start = (bf16[16,6,256]{2,0,1:T(8,128)(2,1)S(1)}, bf16[16,6,256]{2,0,1:T(8,128)(2,1)S(1)}, u32[]{:S(2)}, u32[]{:S(2)}) collective-permute-start(bf16[16,6,256]{2,0,1:T(8,128)(2,1)S(1)} %get-tuple-element.723), channel_id=1, source_target_pairs={{0,1},{1,2},{2,3},{4,5},{5,6},{6,7},{8,9},{9,10},{10,11},{12,13},{... | collective-permute-start | bytes 147464 | tf_op jit(solution)/shard_map/ppermute | solution.py:25
  7.7 25.6 %collective-permute-start.2 = (bf16[16,76,268]{2,0,1:T(8,128)(2,1)S(1)}, bf16[16,76,268]{2,0,1:T(8,128)(2,1)S(1)}, u32[]{:S(2)}, u32[]{:S(2)}) collective-permute-start(bf16[16,76,268]{2,0,1:T(8,128)(2,1)S(1)} %fusion.359), channel_id=1, source_target_pairs={{4,0},{8,4},{12,8},{5,1},{9,5},{13,9},{6,2},{10,6},{14,10},{7,3},{... | collective-permute-start | bytes 1955336 | tf_op jit(solution)/shard_map/ppermute | solution.py:37
  10.4 185.8 %collective-permute-start.4 = (f32[1,256]{1,0:T(1,128)}, f32[1,256]{1,0:T(1,128)}, u32[]{:S(2)}, u32[]{:S(2)}) collective-permute-start(f32[1,256]{1,0:T(1,128)} %get-tuple-element.736), channel_id=1, source_target_pairs={{1,0},{2,1},{3,2},{5,4},{6,5},{7,6},{9,8},{10,9},{11,10},{13,12},{... | collective-permute-start | bytes 3080 | tf_op jit(solution)/shard_map/ppermute | solution.py:27
  11.6 184.5 %collective-permute-start.6 = (f32[1,256]{1,0:T(1,128)}, f32[1,256]{1,0:T(1,128)}, u32[]{:S(2)}, u32[]{:S(2)}) collective-permute-start(f32[1,256]{1,0:T(1,128)} %get-tuple-element.735), channel_id=1, source_target_pairs={{0,1},{1,2},{2,3},{4,5},{5,6},{6,7},{8,9},{9,10},{10,11},{12,13},{... | collective-permute-start | bytes 3080 | tf_op jit(solution)/shard_map/ppermute | solution.py:25
  124.5 135.7 %copy-start.1 = (f32[2,4,16,256]{3,2,1,0:T(8,128)}, f32[2,4,16,256]{3,2,1,0:T(8,128)S(1)}, u32[]{:S(2)}) copy-start(f32[2,4,16,256]{3,2,1,0:T(8,128)S(1)} %copy.22) | copy-start | bytes 393220
  124.8 69.9 %copy-start.6 = (f32[4]{0:T(128)S(1)}, f32[4]{0:T(128)}, u32[]{:S(2)}) copy-start(f32[4]{0:T(128)} %get-tuple-element.701) | copy-start | bytes 52
  124.8 69.9 %copy-start.7 = (f32[3]{0:T(128)S(1)}, f32[3]{0:T(128)}, u32[]{:S(2)}) copy-start(f32[3]{0:T(128)} %slice_reduce_fusion) | copy-start | bytes 40
  124.8 71.3 %copy-start.3 = (f32[64,256]{1,0:T(8,128)S(1)}, f32[64,256]{1,0:T(8,128)}, u32[]{:S(2)}) copy-start(f32[64,256]{1,0:T(8,128)} %copy-done.2) | copy-start | bytes 196612
  190.3 10.3 %collective-permute-start.3 = (f32[2,2,64,256]{3,2,1,0:T(8,128)S(1)}, f32[2,2,64,256]{3,2,1,0:T(8,128)S(1)}, u32[]{:S(2)}, u32[]{:S(2)}) collective-permute-start(f32[2,2,64,256]{3,2,1,0:T(8,128)S(1)} %pad_maximum_fusion), channel_id=1, source_target_pairs={{0,4},{4,8},{8,12},{1,5},{5,9},{9,13},{2,6},{6,10},{10,14},{3,7},{... | collective-permute-start | bytes 786440 | tf_op jit(solution)/shard_map/ppermute | solution.py:37
  217.7 11.0 %collective-permute-start.5 = (f32[2,1,256]{2,1,0:T(1,128)S(1)}, f32[2,1,256]{2,1,0:T(1,128)S(1)}, u32[]{:S(2)}, u32[]{:S(2)}) collective-permute-start(f32[2,1,256]{2,1,0:T(1,128)S(1)} %get-tuple-element.732), channel_id=1, source_target_pairs={{1,0},{2,1},{3,2},{5,4},{6,5},{7,6},{9,8},{10,9},{11,10},{13,12},{... | collective-permute-start | bytes 6152 | tf_op jit(solution)/shard_map/ppermute | solution.py:27
  219.0 9.7 %collective-permute-start.7 = (f32[2,1,256]{2,1,0:T(1,128)S(1)}, f32[2,1,256]{2,1,0:T(1,128)S(1)}, u32[]{:S(2)}, u32[]{:S(2)}) collective-permute-start(f32[2,1,256]{2,1,0:T(1,128)S(1)} %get-tuple-element.731), channel_id=1, source_target_pairs={{0,1},{1,2},{2,3},{4,5},{5,6},{6,7},{8,9},{9,10},{10,11},{12,13},{... | collective-permute-start | bytes 6152 | tf_op jit(solution)/shard_map/ppermute | solution.py:25
  222.8 6.2 %collective-permute-start.8 = (bf16[2,64,256]{2,1,0:T(8,128)(2,1)S(1)}, bf16[2,64,256]{2,1,0:T(8,128)(2,1)S(1)}, u32[]{:S(2)}, u32[]{:S(2)}) collective-permute-start(bf16[2,64,256]{2,1,0:T(8,128)(2,1)S(1)} %get-tuple-element.699), channel_id=1, source_target_pairs={{4,0},{8,4},{12,8},{5,1},{9,5},{13,9},{6,2},{10,6},{14,10},{7,3},{... | collective-permute-start | bytes 196616 | tf_op jit(solution)/shard_map/ppermute | solution.py:37
  224.1 6.4 %collective-permute-start.9 = (bf16[2,64,256]{2,1,0:T(8,128)(2,1)S(1)}, bf16[2,64,256]{2,1,0:T(8,128)(2,1)S(1)}, u32[]{:S(2)}, u32[]{:S(2)}) collective-permute-start(bf16[2,64,256]{2,1,0:T(8,128)(2,1)S(1)} %get-tuple-element.699), channel_id=1, source_target_pairs={{0,4},{4,8},{8,12},{1,5},{5,9},{9,13},{2,6},{6,10},{10,14},{3,7},{... | collective-permute-start | bytes 196616 | tf_op jit(solution)/shard_map/ppermute | solution.py:37
  231.6 10.5 %collective-permute-start.10 = (f32[2,1,256]{2,1,0:T(1,128)S(1)}, f32[2,1,256]{2,1,0:T(1,128)S(1)}, u32[]{:S(2)}, u32[]{:S(2)}) collective-permute-start(f32[2,1,256]{2,1,0:T(1,128)S(1)} %get-tuple-element.730), channel_id=1, source_target_pairs={{1,0},{2,1},{3,2},{5,4},{6,5},{7,6},{9,8},{10,9},{11,10},{13,12},{... | collective-permute-start | bytes 6152 | tf_op jit(solution)/shard_map/ppermute | solution.py:27
  232.9 9.3 %collective-permute-start.11 = (f32[2,1,256]{2,1,0:T(1,128)S(1)}, f32[2,1,256]{2,1,0:T(1,128)S(1)}, u32[]{:S(2)}, u32[]{:S(2)}) collective-permute-start(f32[2,1,256]{2,1,0:T(1,128)S(1)} %get-tuple-element.729), channel_id=1, source_target_pairs={{0,1},{1,2},{2,3},{4,5},{5,6},{6,7},{8,9},{9,10},{10,11},{12,13},{... | collective-permute-start | bytes 6152 | tf_op jit(solution)/shard_map/ppermute | solution.py:25
  236.0 6.5 %collective-permute-start.12 = (bf16[2,64,256]{2,1,0:T(8,128)(2,1)S(1)}, bf16[2,64,256]{2,1,0:T(8,128)(2,1)S(1)}, u32[]{:S(2)}, u32[]{:S(2)}) collective-permute-start(bf16[2,64,256]{2,1,0:T(8,128)(2,1)S(1)} %get-tuple-element.697), channel_id=1, source_target_pairs={{4,0},{8,4},{12,8},{5,1},{9,5},{13,9},{6,2},{10,6},{14,10},{7,3},{... | collective-permute-start | bytes 196616 | tf_op jit(solution)/shard_map/ppermute | solution.py:37
  237.3 6.8 %collective-permute-start.13 = (bf16[2,64,256]{2,1,0:T(8,128)(2,1)S(1)}, bf16[2,64,256]{2,1,0:T(8,128)(2,1)S(1)}, u32[]{:S(2)}, u32[]{:S(2)}) collective-permute-start(bf16[2,64,256]{2,1,0:T(8,128)(2,1)S(1)} %get-tuple-element.697), channel_id=1, source_target_pairs={{0,4},{4,8},{8,12},{1,5},{5,9},{9,13},{2,6},{6,10},{10,14},{3,7},{... | collective-permute-start | bytes 196616 | tf_op jit(solution)/shard_map/ppermute | solution.py:37
  245.2 9.9 %collective-permute-start.14 = (f32[2,1,256]{2,1,0:T(1,128)S(1)}, f32[2,1,256]{2,1,0:T(1,128)S(1)}, u32[]{:S(2)}, u32[]{:S(2)}) collective-permute-start(f32[2,1,256]{2,1,0:T(1,128)S(1)} %get-tuple-element.728), channel_id=1, source_target_pairs={{1,0},{2,1},{3,2},{5,4},{6,5},{7,6},{9,8},{10,9},{11,10},{13,12},{... | collective-permute-start | bytes 6152 | tf_op jit(solution)/shard_map/ppermute | solution.py:27
  246.5 8.6 %collective-permute-start.15 = (f32[2,1,256]{2,1,0:T(1,128)S(1)}, f32[2,1,256]{2,1,0:T(1,128)S(1)}, u32[]{:S(2)}, u32[]{:S(2)}) collective-permute-start(f32[2,1,256]{2,1,0:T(1,128)S(1)} %get-tuple-element.727), channel_id=1, source_target_pairs={{0,1},{1,2},{2,3},{4,5},{5,6},{6,7},{8,9},{9,10},{10,11},{12,13},{... | collective-permute-start | bytes 6152 | tf_op jit(solution)/shard_map/ppermute | solution.py:25
  249.5 6.2 %collective-permute-start.17 = (bf16[2,64,256]{2,1,0:T(8,128)(2,1)S(1)}, bf16[2,64,256]{2,1,0:T(8,128)(2,1)S(1)}, u32[]{:S(2)}, u32[]{:S(2)}) collective-permute-start(bf16[2,64,256]{2,1,0:T(8,128)(2,1)S(1)} %get-tuple-element.695), channel_id=1, source_target_pairs={{0,4},{4,8},{8,12},{1,5},{5,9},{9,13},{2,6},{6,10},{10,14},{3,7},{... | collective-permute-start | bytes 196616 | tf_op jit(solution)/shard_map/ppermute | solution.py:37
  253.8 6.2 %collective-permute-start.16 = (bf16[2,64,256]{2,1,0:T(8,128)(2,1)S(1)}, bf16[2,64,256]{2,1,0:T(8,128)(2,1)S(1)}, u32[]{:S(2)}, u32[]{:S(2)}) collective-permute-start(bf16[2,64,256]{2,1,0:T(8,128)(2,1)S(1)} %get-tuple-element.695), channel_id=1, source_target_pairs={{4,0},{8,4},{12,8},{5,1},{9,5},{13,9},{6,2},{10,6},{14,10},{7,3},{... | collective-permute-start | bytes 196616 | tf_op jit(solution)/shard_map/ppermute | solution.py:37
  (6 other events, 17.9 us)
where the time goes:
time: 263 us; the launch traced here: 262 us
  other arithmetic  136 us (52%)
  starting transfers between devices  47.8 us (18%)
  waiting for transfers between devices  27.1 us (10%)
  loops' own time  18 us (7%)
  blocking collectives  16.1 us (6%)
  local copies, waits for them, and re-layouts  14.9 us (6%)
    reduce_sum x80, other arithmetic, band_scores(): jnp.sum(center_band * window_band[:, shift_row:shift_row + height, shift_...  117 us
    ppermute x8, waiting for transfers between devices, passed_along(): lax.ppermute(value, axis, [(source, source + steps) for source in range(i...  26.2 us
    ppermute x8, starting transfers between devices, passed_along(): lax.ppermute(value, axis, [(source, source + steps) for source in range(i...  23.3 us
    ppermute x5, starting transfers between devices, padded_2(): lax.ppermute(tail, axis, [(i, (i + 1) % count) for i in range(ends)])  18.1 us
    another operation x2, loops' own time, flow_of(): lax.map(one_band, jnp.arange(height // band_rows, dtype=jnp.int32))  17.9 us
    all_gather x1, blocking collectives, entering(): everything = lax.all_gather(shard, axis)  16.1 us
    reduce_sum x8, other arithmetic, expected(): flow_row = jnp.sum(weights * row_shift[:, None, None], axis=0) / denominator  8.45 us
    ppermute x5, starting transfers between devices, padded_2(): lax.ppermute(head, axis, [((i + 1) % count, i) for i in range(ends)])  6.45 us
  transfers between devices with their start and end apart: 18, of which 9 were waited for; matrix products, arithmetic and copies ran while one was open for 55% of the time, Pallas kernels for 0%

commit v1 on v0

--- a/solution.py
+++ b/solution.py
@@ -1,8 +1,10 @@
-import math
+import functools
 
 import jax
 import jax.numpy as jnp
 from jax import lax
+from jax.experimental import pallas as pl
+from jax.experimental.pallas import tpu as pltpu
 from jax.sharding import PartitionSpec as P
 
 RADIUS = 6
@@ -54,49 +56,166 @@
     return jax.tree.map(lambda a: a.astype(jnp.bfloat16) if a.dtype == jnp.float32 else a, shard)
 
 
-def expected(stacked):
-    highest = jnp.max(stacked, axis=0)
-    weights = jnp.exp(stacked - highest)
-    denominator = jnp.sum(weights, axis=0)
-    window = 2 * RADIUS + 1
-    places = jnp.arange(window * window, dtype=jnp.int32)
-    row_shift = (places // window - RADIUS).astype(jnp.float32)
-    col_shift = (places % window - RADIUS).astype(jnp.float32)
-    flow_row = jnp.sum(weights * row_shift[:, None, None], axis=0) / denominator
-    flow_col = jnp.sum(weights * col_shift[:, None, None], axis=0) / denominator
-    return jnp.stack([flow_row, flow_col])
-
-
-def band_scores(center_band, window_band, height, breadth):
-    scores = []
-    for shift_row in range(2 * RADIUS + 1):
-        for shift_col in range(2 * RADIUS + 1):
-            scores.append(
-                jnp.sum(
-                    center_band
-                    * window_band[
-                        :, shift_row : shift_row + height, shift_col : shift_col + breadth
-                    ],
-                    axis=0,
+BLOCK = 4
+SPAN = BLOCK + 2 * RADIUS
+GROUP = 32
+LOG2E = 1.4426950408889634
+MASKED = -1e30
+
+
+def flow_kernel(pairs, e_ref, l_ref, f_ref, b_ref, t_ref, bias_ref, o_ref):
+    rows = f_ref.shape[1]
+    channels, breadth = e_ref.shape[1], e_ref.shape[2]
+    groups = rows // GROUP
+    steps = breadth // BLOCK // (2 // groups)
+    wide = t_ref.shape[3]
+    lane = lax.broadcasted_iota(jnp.int32, (8, 128), 1)
+    sub = lax.broadcasted_iota(jnp.int32, (8, 128), 0)
+    qc = lane // GROUP
+    qr = lane % BLOCK
+    col_ok = []
+    for half in range(2):
+        kc = sub + 8 * half
+        col_ok.append((kc >= qc) & (kc <= qc + 2 * RADIUS))
+    edge = [k for k in range(SPAN) if k < BLOCK - 1 or k > 2 * RADIUS]
+    for n, kr in enumerate(edge):
+        row_ok = (qr <= kr) & (kr <= qr + 2 * RADIUS)
+        for half in range(2):
+            bias_ref[2 * n + half] = jnp.where(row_ok & col_ok[half], 0.0, MASKED)
+    place = jnp.where(
+        lax.broadcasted_iota(jnp.int32, (wide, breadth), 0)
+        == lax.broadcasted_iota(jnp.int32, (wide, breadth), 1) + RADIUS,
+        1.0,
+        0.0,
+    ).astype(jnp.bfloat16)
+    per = GROUP // BLOCK
+    for side, ref in enumerate((e_ref, l_ref)):
+        for g in range(groups):
+            for kr in range(0, SPAN, 2):
+                pieces = [
+                    ref[GROUP * g + kr + k + BLOCK * b] for k in range(2) for b in range(per)
+                ]
+                flat = jnp.concatenate(pieces, axis=0)
+                out = lax.dot_general(
+                    place, flat, (((1,), (1,)), ((), ())), preferred_element_type=jnp.float32
                 )
+                t_ref[side, g, kr] = out[:, :128]
+                t_ref[side, g, kr + 1] = out[:, 128:]
+
+    own = lax.broadcasted_iota(jnp.int32, (16, 128), 0) // BLOCK
+    of = lax.broadcasted_iota(jnp.int32, (16, 128), 1) // channels
+    zero_b = jnp.zeros((16, 128), jnp.bfloat16)
+    sub_qr = sub % BLOCK
+    for side in range(2):
+
+        def step(i, carry):
+            tiles = []
+            for k in range(2):
+                g = k if groups == 2 else 0
+                base = i * BLOCK + (0 if groups == 2 else k * (breadth // 2))
+                tiles.append((g, base))
+            keys = []
+            for kr in range(SPAN):
+                keys.append(
+                    jnp.concatenate(
+                        [t_ref[1 - side, g, kr, pl.ds(base, SPAN), :] for g, base in tiles], axis=1
+                    ).astype(jnp.bfloat16)
+                )
+            keys = jnp.concatenate(keys, axis=0)
+            parts = []
+            for k, (g, base) in enumerate(tiles):
+                for c in range(BLOCK):
+                    v = None
+                    for r in range(BLOCK):
+                        row = jnp.broadcast_to(
+                            t_ref[side, g, RADIUS + r, pl.ds(base + RADIUS + c, 1), :], (8, 128)
+                        )
+                        v = row if v is None else jnp.where(sub_qr == r, row, v)
+                    vb = jnp.concatenate([v, v], axis=0).astype(jnp.bfloat16)
+                    for q in range(per // 4):
+                        sel = jnp.where(of == own + 4 * q, vb, zero_b)
+                        parts.append(
+                            jnp.concatenate([sel, zero_b] if k == 0 else [zero_b, sel], axis=1)
+                        )
+            queries = jnp.concatenate(parts, axis=0)
+            scores = lax.dot_general(
+                keys, queries, (((1,), (1,)), ((), ())), preferred_element_type=jnp.float32
             )
-    return score_scale * jnp.stack(scores)
-
-
-def flow_of(center, other):
-    channels, height, breadth = center.shape
-    band_rows = math.gcd(height, 16)
-
-    def one_band(band_index):
-        band_start = band_index * band_rows
-        center_band = lax.dynamic_slice_in_dim(center, band_start, band_rows, 1).astype(jnp.float32)
-        window_band = lax.dynamic_slice_in_dim(other, band_start, band_rows + 2 * RADIUS, 1).astype(
-            jnp.float32
-        )
-        return expected(band_scores(center_band, window_band, band_rows, breadth))
-
-    results = lax.map(one_band, jnp.arange(height // band_rows, dtype=jnp.int32))
-    return jnp.moveaxis(results, 0, 1).reshape(2, height, breadth)
+            for k, (g, base) in enumerate(tiles):
+                s = {}
+                for kr in range(SPAN):
+                    for half in range(2):
+                        s[kr, half] = scores[
+                            SPAN * kr + 8 * half : SPAN * kr + 8 * half + 8, 128 * k : 128 * k + 128
+                        ]
+                for n, kr in enumerate(edge):
+                    for half in range(2):
+                        s[kr, half] = s[kr, half] + bias_ref[2 * n + half]
+                peak = []
+                for half in range(2):
+                    inner = functools.reduce(
+                        jnp.maximum, [s[kr, half] for kr in range(SPAN) if kr not in edge]
+                    )
+                    inner = jnp.where(col_ok[half], inner, MASKED)
+                    peak.append(
+                        functools.reduce(jnp.maximum, [s[kr, half] for kr in edge] + [inner])
+                    )
+                top = jnp.max(jnp.maximum(peak[0], peak[1]), axis=0, keepdims=True)
+                top = jnp.broadcast_to(top, (8, 128))
+                total, slope = [], []
+                for half in range(2):
+                    acc = None
+                    mom = None
+                    for kr in reversed(range(SPAN)):
+                        w = jnp.exp2((s[kr, half] - top) * (LOG2E * score_scale))
+                        acc = w if acc is None else acc + w
+                        if kr > 0:
+                            mom = acc if mom is None else mom + acc
+                    total.append(jnp.where(col_ok[half], acc, 0.0))
+                    slope.append(jnp.where(col_ok[half], mom, 0.0))
+                both = total[0] + total[1]
+                den = jnp.sum(both, axis=0, keepdims=True)
+                row_sum = jnp.sum(slope[0] + slope[1], axis=0, keepdims=True)
+                col_sum = jnp.sum(
+                    both * sub.astype(jnp.float32) + 8.0 * total[1], axis=0, keepdims=True
+                )
+                fr = row_sum / den - (qr[0:1] + RADIUS).astype(jnp.float32)
+                fc = col_sum / den - (qc[0:1] + RADIUS).astype(jnp.float32)
+                both_f = jnp.concatenate([fr, fc], axis=0)
+                for c in range(BLOCK):
+                    r = both_f if c == 0 else pltpu.roll(both_f, 128 - GROUP * c, 1)
+                    o_ref[side, 0, g, pl.ds(base + c, 1), :] = r[0:1]
+                    o_ref[side, 1, g, pl.ds(base + c, 1), :] = r[1:2]
+            return carry
+
+        lax.fori_loop(0, steps, step, 0)
+    for side, ref in enumerate((f_ref, b_ref)):
+        for comp in range(2):
+            for g in range(groups):
+                ref[comp, GROUP * g : GROUP * g + GROUP, :] = jnp.transpose(
+                    o_ref[side, comp, g], (1, 0)
+                )[:GROUP]
+
+
+def flows(early, late):
+    rows = early.shape[0] - 2 * RADIUS
+    channels, breadth = early.shape[1:]
+    groups = rows // GROUP
+    wide = breadth + 16
+    out = jax.ShapeDtypeStruct((2, rows, breadth), jnp.float32)
+    return pl.pallas_call(
+        functools.partial(flow_kernel, None),
+        out_shape=(out, out),
+        in_specs=[pl.BlockSpec(memory_space=pltpu.VMEM)] * 2,
+        out_specs=(pl.BlockSpec(memory_space=pltpu.VMEM),) * 2,
+        scratch_shapes=[
+            pltpu.VMEM((2, groups, SPAN, wide, 128), jnp.float32),
+            pltpu.VMEM((12, 8, 128), jnp.float32),
+            pltpu.VMEM((2, 2, groups, breadth, 128), jnp.float32),
+        ],
+        compiler_params=pltpu.CompilerParams(vmem_limit_bytes=40 * 2**20),
+        name="flows",
+    )(early, late)
 
 
 def widen(values_in, margin):
@@ -132,8 +251,7 @@
 
 
 def on_device(features, class_map, stiffness, valid):
-    center = features[0]
-    height, breadth = (center.shape[1], center.shape[2])
+    center = jnp.transpose(features[0], (1, 0, 2))
     section = lax.axis_index("gz")
     tile_index = lax.axis_index(("xy", "col"))
     column = lax.dynamic_slice_in_dim(valid, tile_index, 1, 1)[:, 0].astype(jnp.float32)
@@ -144,10 +262,9 @@
         lax.dynamic_index_in_dim(link_all, jnp.maximum(section - 1, 0), 0, keepdims=False),
         0.0,
     )
-    padded = widen(padded_2(center, ((("xy", "col"), 1),), RADIUS), RADIUS)
+    padded = padded_2(center, ((("xy", "col"), 0),), RADIUS)
     upper_pad = passed_along(padded, "gz", -1)
-    forward = flow_of(center, upper_pad)
-    ahead_flow = flow_of(upper_pad[:, RADIUS : RADIUS + height, RADIUS : RADIUS + breadth], padded)
+    forward, ahead_flow = flows(padded, upper_pad)
     passed = passed_along(jnp.stack([forward, ahead_flow]), "gz", 1)
     prior_flow = passed[0]
     backward = passed[1]

time: 263 us -> 148 us (0.56)
  other arithmetic: 136 us -> 6.33 us
  Pallas kernels: 0 us -> 50.7 us
  loops' own time: 18 us -> 0.08 us
  local copies, waits for them, and re-layouts: 14.9 us -> 2.79 us
  waiting for transfers between devices: 27.1 us -> 21.6 us
    reduce_sum x88 -> x0, other arithmetic: 125 us -> none  [the longest x80 117 us: band_scores(): jnp.sum(center_band * window_band[:, shift_row:shift_row + height, shift_...]
    pallas_call x0 -> x1, Pallas kernels: none -> 50.7 us  [flows(): pl.pallas_call(functools.partial(flow_kernel, None), out_shape=(out, out)...]
    another operation x2 -> x0, loops' own time: 17.9 us -> none  [flow_of(): lax.map(one_band, jnp.arange(height // band_rows, dtype=jnp.int32))]
    ppermute x8, waiting for transfers between devices: 26.2 us -> 17.6 us  [passed_along(): lax.ppermute(value, axis, [(source, source + steps) for source in range(i...]
    dynamic_slice x20 -> x0, local copies, waits for them, and re-layouts: 5.73 us -> none  [the longest x8 5.33 us: flow_of(): lax.map(one_band, jnp.arange(height // band_rows, dtype=jnp.int32))]
    while x1352 -> x0, local copies, waits for them, and re-layouts: 4.97 us -> none
    ppermute x5, waiting for transfers between devices: 0.01 us -> 3.92 us  [padded_2(): lax.ppermute(head, axis, [((i + 1) % count, i) for i in range(ends)])]
  transfers between devices with their start and end apart: 18 -> 18, of which waited for: 9 -> 9; matrix products, arithmetic and copies ran while one was open for 55% -> 2% of each run, Pallas kernels for 0% -> 34%
where the time goes in v1:
time: 148 us; the launch traced here: 147 us
  Pallas kernels  50.7 us (34%)
  starting transfers between devices  46.5 us (31%)
  waiting for transfers between devices  21.6 us (15%)
  blocking collectives  17.3 us (12%)
  other arithmetic  6.33 us (4%)
  local copies, waits for them, and re-layouts  2.79 us (2%)
  between operations  1.73 us (1%)
    pallas_call x1, Pallas kernels, flows(): pl.pallas_call(functools.partial(flow_kernel, None), out_shape=(out, out)...  50.7 us
    ppermute x8, starting transfers between devices, passed_along(): lax.ppermute(value, axis, [(source, source + steps) for source in range(i...  23.1 us
    ppermute x8, waiting for transfers between devices, passed_along(): lax.ppermute(value, axis, [(source, source + steps) for source in range(i...  17.6 us
    all_gather x1, blocking collectives, entering(): everything = lax.all_gather(shard, axis)  17.3 us
    ppermute x5, starting transfers between devices, padded_2(): lax.ppermute(tail, axis, [(i, (i + 1) % count) for i in range(ends)])  16.8 us
    ppermute x5, starting transfers between devices, padded_2(): lax.ppermute(head, axis, [((i + 1) % count, i) for i in range(ends)])  6.59 us
    ppermute x5, waiting for transfers between devices, padded_2(): lax.ppermute(head, axis, [((i + 1) % count, i) for i in range(ends)])  3.92 us
  transfers between devices with their start and end apart: 18, of which 9 were waited for; matrix products, arithmetic and copies ran while one was open for 2% of the time, Pallas kernels for 34%

profile of v1, /device:TPU:0, one launch (start us, length us, event | category | flops | bytes accessed | tf_op | source)
XLA Modules:
  0.0 147.1 jit_solution(1407731890238831154)
XLA Ops:
  0.6 1.3 copy.10
  2.0 2.4 %collective-permute-start = (bf16[6,16,256]{2,1,0:T(8,128)(2,1)S(1)}, bf16[6,16,256]{2,1,0:T(8,128)(2,1)S(1)}, u32[]{:S(2)}, u32[]{:S(2)}) collective-permute-start(bf16[6,16,256]{2,1,0:T(8,128)(2,1)S(1)} %get-tuple-element.135), channel_id=1, source_target_pairs={{0,1},{1,2},{2,3},{4,5},{5,6},{6,7},{8,9},{9,10},{10,11},{12,13},{... | collective-permute-start | bytes 147464 | tf_op jit(solution)/shard_map/ppermute | solution.py:27
  4.4 1.4 collective-permute-start.1
  5.8 3.9 %collective-permute-done.1 = bf16[6,16,256]{2,1,0:T(8,128)(2,1)S(1)} collective-permute-done((bf16[6,16,256]{2,1,0:T(8,128)(2,1)S(1)}, bf16[6,16,256]{2,1,0:T(8,128)(2,1)S(1)}, u32[]{:S(2)}, u32[]{:S(2)}) %collective-permute-start.1) | collective-permute-done | bytes 49184 | tf_op jit(solution)/shard_map/ppermute | solution.py:29
  9.8 1.3 collective-permute-start.2
  11.3 1.3 collective-permute-start.4
  12.6 5.3 %collective-permute-start.6 = (f32[1,256]{1,0:T(1,128)S(1)}, f32[1,256]{1,0:T(1,128)S(1)}, u32[]{:S(2)}, u32[]{:S(2)}) collective-permute-start(f32[1,256]{1,0:T(1,128)S(1)} %get-tuple-element.147), channel_id=1, source_target_pairs={{0,1},{1,2},{2,3},{4,5},{5,6},{6,7},{8,9},{9,10},{10,11},{12,13},{... | collective-permute-start | bytes 3080 | tf_op jit(solution)/shard_map/ppermute | solution.py:27
  18.9 7.9 %collective-permute-done.2.l_ref = bf16[76,16,256]{2,1,0:T(8,128)(2,1)S(1)} collective-permute-done((bf16[76,16,256]{2,1,0:T(8,128)(2,1)S(1)}, bf16[76,16,256]{2,1,0:T(8,128)(2,1)S(1)}, u32[]{:S(2)}, u32[]{:S(2)}) %collective-permute-start.2) | collective-permute-done | bytes 622624 | tf_op jit(solution)/shard_map/ppermute | solution.py:39
  26.8 50.7 %flows.1 = (f32[2,64,256]{2,1,0:T(8,128)}, f32[2,64,256]{2,1,0:T(8,128)S(1)}) custom-call(bf16[76,16,256]{2,1,0:T(8,128)(2,1)S(1)} %pad_maximum_fusion.e_ref, bf16[76,16,256]{2,1,0:T(8,128)(2,1)S(1)} %collective-permute-done.2.l_ref), custom_call_target="tpu_custom_call" | custom-call | tf_op jit(solution)/shard_map/flows/pallas_call | solution.py:206
  78.5 3.6 %collective-permute-start.3 = (f32[2,2,64,256]{3,2,1,0:T(8,128)S(1)}, f32[2,2,64,256]{3,2,1,0:T(8,128)S(1)}, u32[]{:S(2)}, u32[]{:S(2)}) collective-permute-start(f32[2,2,64,256]{3,2,1,0:T(8,128)S(1)} %pad_maximum_fusion.1), channel_id=1, source_target_pairs={{0,4},{4,8},{8,12},{1,5},{5,9},{9,13},{2,6},{6,10},{10,14},{3,7},{... | collective-permute-start | bytes 786440 | tf_op jit(solution)/shard_map/ppermute | solution.py:39
  83.6 4.5 %collective-permute-done.3 = f32[2,2,64,256]{3,2,1,0:T(8,128)S(1)} collective-permute-done((f32[2,2,64,256]{3,2,1,0:T(8,128)S(1)}, f32[2,2,64,256]{3,2,1,0:T(8,128)S(1)}, u32[]{:S(2)}, u32[]{:S(2)}) %collective-permute-start.3) | collective-permute-done | bytes 262176 | tf_op jit(solution)/shard_map/ppermute | solution.py:39
  88.7 17.3 %all-gather = f32[8,64,256]{2,1,0:T(8,128)S(1)} all-gather(f32[2,64,256]{2,1,0:T(8,128)S(1)} %multiply_subtract_fusion), channel_id=2, replica_groups=mesh['groups'=2,'gz'=4,'xy'=2,'col'=2] {'gz'}, dimensions={0}, use_global_device_ids=true | all-gather | bytes 655360 | tf_op jit(solution)/shard_map/all_gather | solution.py:44
  107.6 3.0 %collective-permute-start.7 = (f32[2,1,256]{2,1,0:T(1,128)S(1)}, f32[2,1,256]{2,1,0:T(1,128)S(1)}, u32[]{:S(2)}, u32[]{:S(2)}) collective-permute-start(f32[2,1,256]{2,1,0:T(1,128)S(1)} %get-tuple-element.143), channel_id=1, source_target_pairs={{0,1},{1,2},{2,3},{4,5},{5,6},{6,7},{8,9},{9,10},{10,11},{12,13},{... | collective-permute-start | bytes 6152 | tf_op jit(solution)/shard_map/ppermute | solution.py:27
  112.0 4.5 %collective-permute-start.9 = (bf16[2,64,256]{2,1,0:T(8,128)(2,1)S(1)}, bf16[2,64,256]{2,1,0:T(8,128)(2,1)S(1)}, u32[]{:S(2)}, u32[]{:S(2)}) collective-permute-start(bf16[2,64,256]{2,1,0:T(8,128)(2,1)S(1)} %get-tuple-element.131), channel_id=1, source_target_pairs={{0,4},{4,8},{8,12},{1,5},{5,9},{9,13},{2,6},{6,10},{10,14},{3,7},{... | collective-permute-start | bytes 196616 | tf_op jit(solution)/shard_map/ppermute | solution.py:39
  116.9 1.6 %collective-permute-done.9 = bf16[2,64,256]{2,1,0:T(8,128)(2,1)S(1)} collective-permute-done((bf16[2,64,256]{2,1,0:T(8,128)(2,1)S(1)}, bf16[2,64,256]{2,1,0:T(8,128)(2,1)S(1)}, u32[]{:S(2)}, u32[]{:S(2)}) %collective-permute-start.9) | collective-permute-done | bytes 65568 | tf_op jit(solution)/shard_map/ppermute | solution.py:39
  120.8 3.0 %collective-permute-start.11 = (f32[2,1,256]{2,1,0:T(1,128)S(1)}, f32[2,1,256]{2,1,0:T(1,128)S(1)}, u32[]{:S(2)}, u32[]{:S(2)}) collective-permute-start(f32[2,1,256]{2,1,0:T(1,128)S(1)} %get-tuple-element.141), channel_id=1, source_target_pairs={{0,1},{1,2},{2,3},{4,5},{5,6},{6,7},{8,9},{9,10},{10,11},{12,13},{... | collective-permute-start | bytes 6152 | tf_op jit(solution)/shard_map/ppermute | solution.py:27
  125.1 4.9 %collective-permute-start.13 = (bf16[2,64,256]{2,1,0:T(8,128)(2,1)S(1)}, bf16[2,64,256]{2,1,0:T(8,128)(2,1)S(1)}, u32[]{:S(2)}, u32[]{:S(2)}) collective-permute-start(bf16[2,64,256]{2,1,0:T(8,128)(2,1)S(1)} %get-tuple-element.129), channel_id=1, source_target_pairs={{0,4},{4,8},{8,12},{1,5},{5,9},{9,13},{2,6},{6,10},{10,14},{3,7},{... | collective-permute-start | bytes 196616 | tf_op jit(solution)/shard_map/ppermute | solution.py:39
  130.4 1.6 %collective-permute-done.13 = bf16[2,64,256]{2,1,0:T(8,128)(2,1)S(1)} collective-permute-done((bf16[2,64,256]{2,1,0:T(8,128)(2,1)S(1)}, bf16[2,64,256]{2,1,0:T(8,128)(2,1)S(1)}, u32[]{:S(2)}, u32[]{:S(2)}) %collective-permute-start.13) | collective-permute-done | bytes 65568 | tf_op jit(solution)/shard_map/ppermute | solution.py:39
  133.0 1.3 collective-permute-start.14
  134.3 3.0 %collective-permute-start.15 = (f32[2,1,256]{2,1,0:T(1,128)S(1)}, f32[2,1,256]{2,1,0:T(1,128)S(1)}, u32[]{:S(2)}, u32[]{:S(2)}) collective-permute-start(f32[2,1,256]{2,1,0:T(1,128)S(1)} %get-tuple-element.139), channel_id=1, source_target_pairs={{0,1},{1,2},{2,3},{4,5},{5,6},{6,7},{8,9},{9,10},{10,11},{12,13},{... | collective-permute-start | bytes 6152 | tf_op jit(solution)/shard_map/ppermute | solution.py:27
  137.3 1.3 collective-permute-start.16
  138.6 4.9 %collective-permute-start.17 = (bf16[2,64,256]{2,1,0:T(8,128)(2,1)S(1)}, bf16[2,64,256]{2,1,0:T(8,128)(2,1)S(1)}, u32[]{:S(2)}, u32[]{:S(2)}) collective-permute-start(bf16[2,64,256]{2,1,0:T(8,128)(2,1)S(1)} %get-tuple-element.127), channel_id=1, source_target_pairs={{0,4},{4,8},{8,12},{1,5},{5,9},{9,13},{2,6},{6,10},{10,14},{3,7},{... | collective-permute-start | bytes 196616 | tf_op jit(solution)/shard_map/ppermute | solution.py:39
  143.9 1.5 collective-permute-done.17
  145.6 1.4 fusion.21
  (64 shorter events, 12.4 us)
Async XLA Ops:
  2.0 3.9 %collective-permute-start = (bf16[6,16,256]{2,1,0:T(8,128)(2,1)S(1)}, bf16[6,16,256]{2,1,0:T(8,128)(2,1)S(1)}, u32[]{:S(2)}, u32[]{:S(2)}) collective-permute-start(bf16[6,16,256]{2,1,0:T(8,128)(2,1)S(1)} %get-tuple-element.135), channel_id=1, source_target_pairs={{0,1},{1,2},{2,3},{4,5},{5,6},{6,7},{8,9},{9,10},{10,11},{12,13},{... | collective-permute-start | bytes 147464 | tf_op jit(solution)/shard_map/ppermute | solution.py:27
  4.4 6.8 %copy-start.1 = (s32[1,64,256]{2,1,0:T(8,128)S(1)}, s32[1,64,256]{2,1,0:T(8,128)}, u32[]{:S(2)}) copy-start(s32[1,64,256]{2,1,0:T(8,128)} %param.7) | copy-start | bytes 196612
  4.4 5.3 %collective-permute-start.1 = (bf16[6,16,256]{2,1,0:T(8,128)(2,1)S(1)}, bf16[6,16,256]{2,1,0:T(8,128)(2,1)S(1)}, u32[]{:S(2)}, u32[]{:S(2)}) collective-permute-start(bf16[6,16,256]{2,1,0:T(8,128)(2,1)S(1)} %get-tuple-element.136), channel_id=1, source_target_pairs={{1,0},{2,1},{3,2},{5,4},{6,5},{7,6},{9,8},{10,9},{11,10},{13,12},{... | collective-permute-start | bytes 147464 | tf_op jit(solution)/shard_map/ppermute | solution.py:29
  9.8 1.3 copy-start.3
  9.8 17.0 %collective-permute-start.2 = (bf16[76,16,256]{2,1,0:T(8,128)(2,1)S(1)}, bf16[76,16,256]{2,1,0:T(8,128)(2,1)S(1)}, u32[]{:S(2)}, u32[]{:S(2)}) collective-permute-start(bf16[76,16,256]{2,1,0:T(8,128)(2,1)S(1)} %pad_maximum_fusion.e_ref), channel_id=1, source_target_pairs={{4,0},{8,4},{12,8},{5,1},{9,5},{13,9},{6,2},{10,6},{14,10},{7,3},{... | collective-permute-start | bytes 1867784 | tf_op jit(solution)/shard_map/ppermute | solution.py:39
  11.3 72.2 %collective-permute-start.4 = (f32[1,256]{1,0:T(1,128)S(1)}, f32[1,256]{1,0:T(1,128)S(1)}, u32[]{:S(2)}, u32[]{:S(2)}) collective-permute-start(f32[1,256]{1,0:T(1,128)S(1)} %get-tuple-element.148), channel_id=1, source_target_pairs={{1,0},{2,1},{3,2},{5,4},{6,5},{7,6},{9,8},{10,9},{11,10},{13,12},{... | collective-permute-start | bytes 3080 | tf_op jit(solution)/shard_map/ppermute | solution.py:29
  12.6 70.9 %collective-permute-start.6 = (f32[1,256]{1,0:T(1,128)S(1)}, f32[1,256]{1,0:T(1,128)S(1)}, u32[]{:S(2)}, u32[]{:S(2)}) collective-permute-start(f32[1,256]{1,0:T(1,128)S(1)} %get-tuple-element.147), channel_id=1, source_target_pairs={{0,1},{1,2},{2,3},{4,5},{5,6},{6,7},{8,9},{9,10},{10,11},{12,13},{... | collective-permute-start | bytes 3080 | tf_op jit(solution)/shard_map/ppermute | solution.py:27
  17.9 0.7 copy-start.2
  78.5 9.6 %copy-start = (f32[2,64,256]{2,1,0:T(8,128)S(1)}, f32[2,64,256]{2,1,0:T(8,128)}, u32[]{:S(2)}) copy-start(f32[2,64,256]{2,1,0:T(8,128)} %get-tuple-element.83) | copy-start | bytes 393220
  78.5 9.6 %collective-permute-start.3 = (f32[2,2,64,256]{3,2,1,0:T(8,128)S(1)}, f32[2,2,64,256]{3,2,1,0:T(8,128)S(1)}, u32[]{:S(2)}, u32[]{:S(2)}) collective-permute-start(f32[2,2,64,256]{3,2,1,0:T(8,128)S(1)} %pad_maximum_fusion.1), channel_id=1, source_target_pairs={{0,4},{4,8},{8,12},{1,5},{5,9},{9,13},{2,6},{6,10},{10,14},{3,7},{... | collective-permute-start | bytes 786440 | tf_op jit(solution)/shard_map/ppermute | solution.py:39
  106.3 10.3 %collective-permute-start.5 = (f32[2,1,256]{2,1,0:T(1,128)S(1)}, f32[2,1,256]{2,1,0:T(1,128)S(1)}, u32[]{:S(2)}, u32[]{:S(2)}) collective-permute-start(f32[2,1,256]{2,1,0:T(1,128)S(1)} %get-tuple-element.144), channel_id=1, source_target_pairs={{1,0},{2,1},{3,2},{5,4},{6,5},{7,6},{9,8},{10,9},{11,10},{13,12},{... | collective-permute-start | bytes 6152 | tf_op jit(solution)/shard_map/ppermute | solution.py:29
  107.6 9.0 %collective-permute-start.7 = (f32[2,1,256]{2,1,0:T(1,128)S(1)}, f32[2,1,256]{2,1,0:T(1,128)S(1)}, u32[]{:S(2)}, u32[]{:S(2)}) collective-permute-start(f32[2,1,256]{2,1,0:T(1,128)S(1)} %get-tuple-element.143), channel_id=1, source_target_pairs={{0,1},{1,2},{2,3},{4,5},{5,6},{6,7},{8,9},{9,10},{10,11},{12,13},{... | collective-permute-start | bytes 6152 | tf_op jit(solution)/shard_map/ppermute | solution.py:27
  110.7 6.2 %collective-permute-start.8 = (bf16[2,64,256]{2,1,0:T(8,128)(2,1)S(1)}, bf16[2,64,256]{2,1,0:T(8,128)(2,1)S(1)}, u32[]{:S(2)}, u32[]{:S(2)}) collective-permute-start(bf16[2,64,256]{2,1,0:T(8,128)(2,1)S(1)} %get-tuple-element.131), channel_id=1, source_target_pairs={{4,0},{8,4},{12,8},{5,1},{9,5},{13,9},{6,2},{10,6},{14,10},{7,3},{... | collective-permute-start | bytes 196616 | tf_op jit(solution)/shard_map/ppermute | solution.py:39
  112.0 6.4 %collective-permute-start.9 = (bf16[2,64,256]{2,1,0:T(8,128)(2,1)S(1)}, bf16[2,64,256]{2,1,0:T(8,128)(2,1)S(1)}, u32[]{:S(2)}, u32[]{:S(2)}) collective-permute-start(bf16[2,64,256]{2,1,0:T(8,128)(2,1)S(1)} %get-tuple-element.131), channel_id=1, source_target_pairs={{0,4},{4,8},{8,12},{1,5},{5,9},{9,13},{2,6},{6,10},{10,14},{3,7},{... | collective-permute-start | bytes 196616 | tf_op jit(solution)/shard_map/ppermute | solution.py:39
  119.5 10.5 %collective-permute-start.10 = (f32[2,1,256]{2,1,0:T(1,128)S(1)}, f32[2,1,256]{2,1,0:T(1,128)S(1)}, u32[]{:S(2)}, u32[]{:S(2)}) collective-permute-start(f32[2,1,256]{2,1,0:T(1,128)S(1)} %get-tuple-element.142), channel_id=1, source_target_pairs={{1,0},{2,1},{3,2},{5,4},{6,5},{7,6},{9,8},{10,9},{11,10},{13,12},{... | collective-permute-start | bytes 6152 | tf_op jit(solution)/shard_map/ppermute | solution.py:29
  120.8 9.3 %collective-permute-start.11 = (f32[2,1,256]{2,1,0:T(1,128)S(1)}, f32[2,1,256]{2,1,0:T(1,128)S(1)}, u32[]{:S(2)}, u32[]{:S(2)}) collective-permute-start(f32[2,1,256]{2,1,0:T(1,128)S(1)} %get-tuple-element.141), channel_id=1, source_target_pairs={{0,1},{1,2},{2,3},{4,5},{5,6},{6,7},{8,9},{9,10},{10,11},{12,13},{... | collective-permute-start | bytes 6152 | tf_op jit(solution)/shard_map/ppermute | solution.py:27
  123.8 6.5 %collective-permute-start.12 = (bf16[2,64,256]{2,1,0:T(8,128)(2,1)S(1)}, bf16[2,64,256]{2,1,0:T(8,128)(2,1)S(1)}, u32[]{:S(2)}, u32[]{:S(2)}) collective-permute-start(bf16[2,64,256]{2,1,0:T(8,128)(2,1)S(1)} %get-tuple-element.129), channel_id=1, source_target_pairs={{4,0},{8,4},{12,8},{5,1},{9,5},{13,9},{6,2},{10,6},{14,10},{7,3},{... | collective-permute-start | bytes 196616 | tf_op jit(solution)/shard_map/ppermute | solution.py:39
  125.1 6.8 %collective-permute-start.13 = (bf16[2,64,256]{2,1,0:T(8,128)(2,1)S(1)}, bf16[2,64,256]{2,1,0:T(8,128)(2,1)S(1)}, u32[]{:S(2)}, u32[]{:S(2)}) collective-permute-start(bf16[2,64,256]{2,1,0:T(8,128)(2,1)S(1)} %get-tuple-element.129), channel_id=1, source_target_pairs={{0,4},{4,8},{8,12},{1,5},{5,9},{9,13},{2,6},{6,10},{10,14},{3,7},{... | collective-permute-start | bytes 196616 | tf_op jit(solution)/shard_map/ppermute | solution.py:39
  133.0 10.5 %collective-permute-start.14 = (f32[2,1,256]{2,1,0:T(1,128)S(1)}, f32[2,1,256]{2,1,0:T(1,128)S(1)}, u32[]{:S(2)}, u32[]{:S(2)}) collective-permute-start(f32[2,1,256]{2,1,0:T(1,128)S(1)} %get-tuple-element.140), channel_id=1, source_target_pairs={{1,0},{2,1},{3,2},{5,4},{6,5},{7,6},{9,8},{10,9},{11,10},{13,12},{... | collective-permute-start | bytes 6152 | tf_op jit(solution)/shard_map/ppermute | solution.py:29
  134.3 9.3 %collective-permute-start.15 = (f32[2,1,256]{2,1,0:T(1,128)S(1)}, f32[2,1,256]{2,1,0:T(1,128)S(1)}, u32[]{:S(2)}, u32[]{:S(2)}) collective-permute-start(f32[2,1,256]{2,1,0:T(1,128)S(1)} %get-tuple-element.139), channel_id=1, source_target_pairs={{0,1},{1,2},{2,3},{4,5},{5,6},{6,7},{8,9},{9,10},{10,11},{12,13},{... | collective-permute-start | bytes 6152 | tf_op jit(solution)/shard_map/ppermute | solution.py:27
  137.3 6.6 %collective-permute-start.16 = (bf16[2,64,256]{2,1,0:T(8,128)(2,1)S(1)}, bf16[2,64,256]{2,1,0:T(8,128)(2,1)S(1)}, u32[]{:S(2)}, u32[]{:S(2)}) collective-permute-start(bf16[2,64,256]{2,1,0:T(8,128)(2,1)S(1)} %get-tuple-element.127), channel_id=1, source_target_pairs={{4,0},{8,4},{12,8},{5,1},{9,5},{13,9},{6,2},{10,6},{14,10},{7,3},{... | collective-permute-start | bytes 196616 | tf_op jit(solution)/shard_map/ppermute | solution.py:39
  138.6 6.8 %collective-permute-start.17 = (bf16[2,64,256]{2,1,0:T(8,128)(2,1)S(1)}, bf16[2,64,256]{2,1,0:T(8,128)(2,1)S(1)}, u32[]{:S(2)}, u32[]{:S(2)}) collective-permute-start(bf16[2,64,256]{2,1,0:T(8,128)(2,1)S(1)} %get-tuple-element.127), channel_id=1, source_target_pairs={{0,4},{4,8},{8,12},{1,5},{5,9},{9,13},{2,6},{6,10},{10,14},{3,7},{... | collective-permute-start | bytes 196616 | tf_op jit(solution)/shard_map/ppermute | solution.py:39

commit v2 on v1

v2 whole, which is shorter than its diff:
```python
import functools

import jax
import jax.numpy as jnp
from jax import lax
from jax.experimental import pallas as pl
from jax.experimental.pallas import tpu as pltpu
from jax.sharding import PartitionSpec as P

RADIUS = 6
STEPS = 3
score_scale = 0.25
step_size = 0.1
saturation = 2.0
tile_axes = ("xy", "col")


def shifted(value, axis, steps):
    count = lax.axis_size(axis)
    initial, last = (max(0, -steps), min(count, count - steps))
    return lax.ppermute(value, axis, [(source, source + steps) for source in range(initial, last)])


BLOCK = 4
SPAN = BLOCK + 2 * RADIUS
GROUP = 32
LOG2E = 1.4426950408889634
MASKED = -1e30


def flow_kernel(e_ref, l_ref, f_ref, b_ref, t_ref, bias_ref, o_ref, s0_ref, s1_ref, s2_ref, s3_ref, w_ref):

    rows = f_ref.shape[1]
    channels, breadth = e_ref.shape[1], e_ref.shape[2]
    groups = rows // GROUP
    steps = breadth // BLOCK // (2 // groups)
    wide = t_ref.shape[3]
    lane = lax.broadcasted_iota(jnp.int32, (8, 128), 1)
    sub = lax.broadcasted_iota(jnp.int32, (8, 128), 0)
    qc = lane // GROUP
    qr = lane % GROUP // (GROUP // BLOCK)
    col_ok = []
    for half in range(2):
        kc = sub + 8 * half
        col_ok.append((kc >= qc) & (kc <= qc + 2 * RADIUS))
    edge = [k for k in range(SPAN) if k < BLOCK - 1 or k > 2 * RADIUS]
    for n, kr in enumerate(edge):
        row_ok = (qr <= kr) & (kr <= qr + 2 * RADIUS)
        for half in range(2):
            bias_ref[2 * n + half] = jnp.where(row_ok & col_ok[half], 0.0, MASKED)
    place = jnp.where(
        lax.broadcasted_iota(jnp.int32, (wide, breadth), 0)
        == lax.broadcasted_iota(jnp.int32, (wide, breadth), 1) + RADIUS,
        1.0,
        0.0,
    ).astype(jnp.bfloat16)
    per = GROUP // BLOCK
    for side, ref in enumerate((e_ref, l_ref)):
        for g in range(groups):
            for kr in range(0, SPAN, 2):
                pieces = [
                    ref[GROUP * g + kr + k + BLOCK * b] for k in range(2) for b in range(per)
                ]
                flat = jnp.concatenate(pieces, axis=0)
                out = lax.dot_general(
                    place, flat, (((1,), (1,)), ((), ())), preferred_element_type=jnp.float32
                )
                t_ref[side, g, kr] = out[:, :128]
                t_ref[side, g, kr + 1] = out[:, 128:]

    diagonal = lane // channels == sub
    zero_b = jnp.zeros((16, 128), jnp.bfloat16)
    for side in range(2):

        def tiles_of(i):
            tiles = []
            for k in range(2):
                g = k if groups == 2 else 0
                base = i * BLOCK + (0 if groups == 2 else k * (breadth // 2))
                tiles.append((g, base))
            return tiles

        def score(i, s_ref):
            tiles = tiles_of(i)
            keys = []
            for kr in range(SPAN):
                keys.append(
                    jnp.concatenate(
                        [t_ref[1 - side, g, kr, pl.ds(base, SPAN), :] for g, base in tiles], axis=1
                    ).astype(jnp.bfloat16)
                )
            keys = jnp.concatenate(keys, axis=0)
            parts = []
            for k, (g, base) in enumerate(tiles):
                for c in range(BLOCK):
                    for r in range(0, BLOCK, 2):
                        pair = [
                            jnp.where(
                                diagonal,
                                t_ref[side, g, RADIUS + r + m, pl.ds(base + RADIUS + c, 1), :],
                                0.0,
                            )
                            for m in range(2)
                        ]
                        sel = jnp.concatenate(pair, axis=0).astype(jnp.bfloat16)
                        parts.append(
                            jnp.concatenate([sel, zero_b] if k == 0 else [zero_b, sel], axis=1)
                        )
            queries = jnp.concatenate(parts, axis=0)
            s_ref[...] = lax.dot_general(
                keys, queries, (((1,), (1,)), ((), ())), preferred_element_type=jnp.float32
            )

        def settle(i, s_ref):
            for k, (g, base) in enumerate(tiles_of(i)):
                s = {}
                for kr in range(SPAN):
                    for half in range(2):
                        s[kr, half] = s_ref[
                            SPAN * kr + 8 * half : SPAN * kr + 8 * half + 8, 128 * k : 128 * k + 128
                        ]
                for n, kr in enumerate(edge):
                    for half in range(2):
                        s[kr, half] = s[kr, half] + bias_ref[2 * n + half]
                peak = []
                for half in range(2):
                    inner = functools.reduce(
                        jnp.maximum, [s[kr, half] for kr in range(SPAN) if kr not in edge]
                    )
                    inner = jnp.where(col_ok[half], inner, MASKED)
                    peak.append(
                        functools.reduce(jnp.maximum, [s[kr, half] for kr in edge] + [inner])
                    )
                top = jnp.max(jnp.maximum(peak[0], peak[1]), axis=0, keepdims=True)
                top = jnp.broadcast_to(top, (8, 128))
                total, slope = [], []
                for half in range(2):
                    acc = None
                    mom = None
                    for kr in reversed(range(SPAN)):
                        w = jnp.exp2((s[kr, half] - top) * (LOG2E * score_scale))
                        acc = w if acc is None else acc + w
                        if kr > 0:
                            mom = acc if mom is None else mom + acc
                    total.append(jnp.where(col_ok[half], acc, 0.0))
                    slope.append(jnp.where(col_ok[half], mom, 0.0))
                both = total[0] + total[1]
                den = jnp.sum(both, axis=0, keepdims=True)
                row_sum = jnp.sum(slope[0] + slope[1], axis=0, keepdims=True)
                col_sum = jnp.sum(
                    both * sub.astype(jnp.float32) + 8.0 * total[1], axis=0, keepdims=True
                )
                fr = row_sum / den - (qr[0:1] + RADIUS).astype(jnp.float32)
                fc = col_sum / den - (qc[0:1] + RADIUS).astype(jnp.float32)
                both_f = jnp.concatenate([fr, fc], axis=0)
                for c in range(BLOCK):
                    r = both_f if c == 0 else pltpu.roll(both_f, 128 - GROUP * c, 1)
                    o_ref[side, 0, g, pl.ds(base + c, 1), :] = r[0:1]
                    o_ref[side, 1, g, pl.ds(base + c, 1), :] = r[1:2]

        def step(j, carry):
            last = steps - 1
            score(4 * j + 2, s2_ref)
            settle(4 * j, s0_ref)
            score(4 * j + 3, s3_ref)
            settle(4 * j + 1, s1_ref)
            score(jnp.minimum(4 * j + 4, last), s0_ref)
            settle(4 * j + 2, s2_ref)
            score(jnp.minimum(4 * j + 5, last), s1_ref)
            settle(4 * j + 3, s3_ref)
            return carry

        score(0, s0_ref)
        score(1, s1_ref)
        lax.fori_loop(0, steps // 4, step, 0)
    for side, ref in enumerate((f_ref, b_ref)):
        for comp in range(2):
            for g in range(groups):
                turned = jnp.transpose(o_ref[side, comp, g], (1, 0))
                for t in range(breadth // 128):
                    for r in range(BLOCK):
                        w_ref[side, comp, g, t, pl.ds(r, per, stride=BLOCK), :] = turned[
                            per * r : per * r + per, 128 * t : 128 * t + 128
                        ]
                    ref[comp, GROUP * g : GROUP * g + GROUP, 128 * t : 128 * t + 128] = w_ref[
                        side, comp, g, t
                    ]


def flows(early, late):
    rows = early.shape[0] - 2 * RADIUS
    channels, breadth = early.shape[1:]
    groups = rows // GROUP
    wide = breadth + 16
    out = jax.ShapeDtypeStruct((2, rows, breadth), jnp.float32)
    return pl.pallas_call(
        flow_kernel,
        out_shape=(out, out),
        in_specs=[pl.BlockSpec(memory_space=pltpu.VMEM)] * 2,
        out_specs=(pl.BlockSpec(memory_space=pltpu.VMEM),) * 2,
        scratch_shapes=[
            pltpu.VMEM((2, groups, SPAN, wide, 128), jnp.float32),
            pltpu.VMEM((12, 8, 128), jnp.float32),
            pltpu.VMEM((2, 2, groups, breadth, 128), jnp.float32),
            pltpu.VMEM((SPAN * SPAN, 256), jnp.float32),
            pltpu.VMEM((SPAN * SPAN, 256), jnp.float32),
            pltpu.VMEM((SPAN * SPAN, 256), jnp.float32),
            pltpu.VMEM((SPAN * SPAN, 256), jnp.float32),
            pltpu.VMEM((2, 2, groups, breadth // 128, GROUP, 128), jnp.float32),
        ],
        compiler_params=pltpu.CompilerParams(vmem_limit_bytes=40 * 2**20),
        name="flows",
    )(early, late)


def spring(vector):
    squares = jnp.sum(vector * vector, axis=0, keepdims=True)
    return vector / jnp.sqrt(1.0 + squares / (saturation * saturation))


def relaxed(u, stiff, inside):
    rows = u.shape[1]
    sides = ((0, 0), (0, 0), (1, 1))
    u_wide = jnp.pad(u, sides)
    s_wide = jnp.pad(stiff[None], sides)
    u_mid, s_mid = u[:, 1:-1], stiff[None, 1:-1]
    total = jnp.zeros_like(u_mid)
    for r, c in ((2, 1), (0, 1), (1, 2), (1, 0)):
        row_part, col_part = slice(r, r + rows - 2), slice(c, c + u.shape[2])
        total = total + 0.5 * (s_mid + s_wide[:, row_part, col_part]) * (
            u_mid - u_wide[:, row_part, col_part]
        )
    return jnp.where(inside[None, 1:-1], u_mid - step_size * total, 0.0)


def trim(rows, value):
    return value[..., rows : value.shape[-2] - rows, :]


def force(up, down, here, below, forward, ahead, prior, backward):
    pulls = here * (spring(up - forward) - spring(-up - ahead))
    return step_size * (pulls + below * (spring(down - backward) - spring(-down - prior)))


def prefix(pair_sum):
    count = lax.axis_size("gz")
    reach = 2
    while reach < count - 2:
        pair_sum = pair_sum + shifted(pair_sum, "gz", reach)
        reach *= 2
    return shifted(pair_sum, "gz", 2)


def on_device(features, class_map, stiffness, valid):
    center = jnp.transpose(features[0], (1, 0, 2))
    height, channels, breadth = center.shape
    codes = (class_map[0] + 1).astype(jnp.bfloat16).reshape(-1, channels, breadth)
    section = lax.axis_index("gz")
    tile = lax.axis_index(tile_axes)

    top = jnp.concatenate([center[:RADIUS], codes[:1]])
    bottom = jnp.concatenate([center[-RADIUS:], codes[-1:]])
    before = shifted(bottom, tile_axes, 1)
    after = shifted(top, tile_axes, -1)
    padded = jnp.concatenate([before[:RADIUS], center, after[:RADIUS]])
    own_codes = jnp.concatenate(
        [
            before[RADIUS, -STEPS:],
            codes.reshape(height, breadth),
            after[RADIUS, :STEPS],
        ]
    )
    spare = -own_codes.shape[0] % channels
    packed = jnp.pad(own_codes, ((0, spare), (0, 0))).reshape(-1, channels, breadth)
    upper = shifted(jnp.concatenate([padded, packed]), "gz", -1)
    upper_pad = upper[: padded.shape[0]]
    upper_codes = upper[padded.shape[0] :].reshape(-1, breadth)[: own_codes.shape[0]]
    forward, ahead = flows(padded, upper_pad)

    both = jnp.concatenate([forward, ahead])
    both = jnp.concatenate(
        [
            shifted(both[:, -STEPS:], tile_axes, 1),
            both,
            shifted(both[:, :STEPS], tile_axes, -1),
        ],
        axis=1,
    )
    message = jnp.concatenate([both, own_codes[None].astype(jnp.float32)])
    lower = shifted(message, "gz", 1)
    fwd, ahd = both[:2], both[2:]
    pri, bwd = lower[:2], lower[2:4]

    def stiff_of(code):
        levels = jnp.arange(stiffness.shape[0], dtype=jnp.float32)[:, None, None] + 1.0
        code = code.astype(jnp.float32)
        field = jnp.sum(jnp.where(code[None] == levels, stiffness[:, None, None], 0.0), axis=0)
        return field, code > 0.0

    stiff, inside = stiff_of(own_codes)
    stiff_up, inside_up = stiff_of(upper_codes)
    stiff_down, inside_down = stiff_of(lower[4])

    sound = jnp.pad(valid.astype(jnp.float32), ((1, 1), (1, 1)))
    near = lax.dynamic_slice(sound, (section, tile), (3, 3))
    links = near[:-1] * near[1:]
    by_row = jnp.repeat(
        links, jnp.array([STEPS, height, STEPS]), axis=1, total_repeat_length=height + 2 * STEPS
    )
    below, here = by_row[0][None, :, None], by_row[1][None, :, None]

    gain = here * (fwd - ahd)
    gain_below = below * (pri - bwd)
    start = 0.5 * (prefix(gain + gain_below) + gain_below)
    pull = force(0.5 * gain, -0.5 * gain_below, here, below, fwd, ahd, pri, bwd)
    sent = trim(2, pull).astype(jnp.bfloat16)
    pull_up = shifted(sent, "gz", -1).astype(jnp.float32)
    pull_down = shifted(sent, "gz", 1).astype(jnp.float32)

    start_up = start + 0.5 * gain
    start_down = start - 0.5 * gain_below
    first = relaxed(start, stiff, inside) + trim(1, pull)
    first_up = relaxed(trim(1, start_up), trim(1, stiff_up), trim(1, inside_up)) + pull_up
    first_down = (
        relaxed(trim(1, start_down), trim(1, stiff_down), trim(1, inside_down)) + pull_down
    )
    mid = trim(1, first)
    fields = [trim(2, x) for x in (here, below, fwd, ahd, pri, bwd)]
    second = relaxed(first, trim(1, stiff), trim(1, inside)) + force(
        first_up - mid, first_down - mid, *fields
    )
    change = trim(1, second) - trim(3, start)
    change = change.astype(jnp.bfloat16)
    last_up = trim(3, start_up) + shifted(change, "gz", -1).astype(jnp.float32)
    last_down = trim(3, start_down) + shifted(change, "gz", 1).astype(jnp.float32)
    fields = [trim(1, x) for x in fields]
    mid = trim(1, second)
    third = relaxed(second, trim(2, stiff), trim(2, inside)) + force(
        last_up - mid, last_down - mid, *fields
    )
    return (third[None], forward[None])


def solution(mesh):
    placed = (
        P(("groups", "gz"), None, tile_axes, None),
        P(("groups", "gz"), tile_axes, None),
        P(),
        P("groups", None),
    )
    return jax.shard_map(
        on_device,
        mesh=mesh,
        in_specs=placed,
        out_specs=(P(("groups", "gz"), None, tile_axes, None),) * 2,
        check_vma=False,
    )
```

time: 148 us -> 106 us (0.72)
  Pallas kernels: 50.7 us -> 22.4 us
  waiting for transfers between devices: 21.6 us -> 39.7 us
  blocking collectives: 17.3 us -> 0 us
  starting transfers between devices: 46.5 us -> 31.4 us
  local copies, waits for them, and re-layouts: 2.79 us -> 5.51 us
    pallas_call x1, Pallas kernels: 50.7 us -> 22.4 us  [flows(): pl.pallas_call(flow_kernel, out_shape=(out, out), in_specs=[pl.BlockSpec(...]
    ppermute x18 -> x11, waiting for transfers between devices: 21.6 us -> 39.7 us  [shifted(): lax.ppermute(value, axis, [(source, source + steps) for source in range(i...]
    all_gather x1 -> x0, blocking collectives: 17.3 us -> none  [entering(): everything = lax.all_gather(shard, axis)]
    ppermute x18 -> x11, starting transfers between devices: 46.5 us -> 31.4 us  [shifted(): lax.ppermute(value, axis, [(source, source + steps) for source in range(i...]
    unnamed x9 -> x13, local copies, waits for them, and re-layouts: 2.03 us -> 4.27 us
  transfers between devices with their start and end apart: 18 -> 11, of which waited for: 9 -> 8; matrix products, arithmetic and copies ran while one was open for 2% -> 3% of each run, Pallas kernels for 34% -> 0%
where the time goes in v2:
time: 106 us; the launch traced here: 105 us
  waiting for transfers between devices  39.7 us (37%)
  starting transfers between devices  31.4 us (30%)
  Pallas kernels  22.4 us (21%)
  local copies, waits for them, and re-layouts  5.51 us (5%)
  other arithmetic  5.21 us (5%)
  between operations  1.19 us (1%)
    ppermute x11, waiting for transfers between devices, shifted(): lax.ppermute(value, axis, [(source, source + steps) for source in range(i...  39.7 us
    ppermute x11, starting transfers between devices, shifted(): lax.ppermute(value, axis, [(source, source + steps) for source in range(i...  31.4 us
    pallas_call x1, Pallas kernels, flows(): pl.pallas_call(flow_kernel, out_shape=(out, out), in_specs=[pl.BlockSpec(...  22.4 us
    unnamed x13, local copies, waits for them, and re-layouts  4.27 us
  transfers between devices with their start and end apart: 11, of which 8 were waited for; matrix products, arithmetic and copies ran while one was open for 3% of the time, Pallas kernels for 0%

profile of v2, /device:TPU:0, one launch (start us, length us, event | category | flops | bytes accessed | tf_op | source)
XLA Modules:
  0.0 105.5 jit_solution(11231692372204036389)
XLA Ops:
  0.6 0.8 add_convert_fusion
  1.5 1.3 %copy.14 = bf16[1,16,64,256]{3,1,2,0:T(8,128)(2,1)S(1)} copy(bf16[1,16,64,256]{3,2,1,0:T(8,128)(2,1)} %param.7) | data formatting | bytes 1048576 | tf_op args[0]
  2.9 1.4 %collective-permute-start.1 = (bf16[7,16,256]{2,1,0:T(8,128)(2,1)S(1)}, bf16[7,16,256]{2,1,0:T(8,128)(2,1)S(1)}, u32[]{:S(2)}, u32[]{:S(2)}) collective-permute-start(bf16[7,16,256]{2,1,0:T(8,128)(2,1)S(1)} %pad_maximum_fusion.5), channel_id=1, source_target_pairs={{1,0},{2,1},{3,2},{5,4},{6,5},{7,6},{9,8},{10,9},{11,10},{13,12},{... | collective-permute-start | bytes 172040 | tf_op jit(solution)/shard_map/ppermute | solution.py:21
  4.3 3.0 %collective-permute-start = (bf16[7,16,256]{2,1,0:T(8,128)(2,1)S(1)}, bf16[7,16,256]{2,1,0:T(8,128)(2,1)S(1)}, u32[]{:S(2)}, u32[]{:S(2)}) collective-permute-start(bf16[7,16,256]{2,1,0:T(8,128)(2,1)S(1)} %pad_maximum_fusion.4), channel_id=1, source_target_pairs={{0,1},{1,2},{2,3},{4,5},{5,6},{6,7},{8,9},{9,10},{10,11},{12,13},{... | collective-permute-start | bytes 172040 | tf_op jit(solution)/shard_map/ppermute | solution.py:21
  7.4 0.7 copy-done.2
  10.0 1.3 %collective-permute-start.2 = (bf16[81,16,256]{2,1,0:T(8,128)(2,1)S(1)}, bf16[81,16,256]{2,1,0:T(8,128)(2,1)S(1)}, u32[]{:S(2)}, u32[]{:S(2)}) collective-permute-start(bf16[81,16,256]{2,1,0:T(8,128)(2,1)S(1)} %pad_maximum_fusion), channel_id=1, source_target_pairs={{4,0},{8,4},{12,8},{5,1},{9,5},{13,9},{6,2},{10,6},{14,10},{7,3},{... | collective-permute-start | bytes 1990664 | tf_op jit(solution)/shard_map/ppermute | solution.py:21
  11.6 18.5 %collective-permute-done.2 = bf16[81,16,256]{2,1,0:T(8,128)(2,1)S(1)} collective-permute-done((bf16[81,16,256]{2,1,0:T(8,128)(2,1)S(1)}, bf16[81,16,256]{2,1,0:T(8,128)(2,1)S(1)}, u32[]{:S(2)}, u32[]{:S(2)}) %collective-permute-start.2) | collective-permute-done | bytes 663584 | tf_op jit(solution)/shard_map/ppermute | solution.py:21
  30.2 22.4 %flows.1 = (f32[2,64,256]{2,1,0:T(8,128)}, f32[2,64,256]{2,1,0:T(8,128)S(1)}) custom-call(bf16[76,16,256]{2,1,0:T(8,128)(2,1)S(1)} %pad_maximum_fusion.1.e_ref, bf16[76,16,256]{2,1,0:T(8,128)(2,1)S(1)} %slice.480.l_ref), custom_call_target="tpu_custom_call" | custom-call | tf_op jit(solution)/shard_map/flows/pallas_call | solution.py:196
  52.6 0.9 constant_dynamic-update-slice_fusion.1
  53.5 1.3 %collective-permute-start.4 = (f32[4,3,256]{2,1,0:T(4,128)S(1)}, f32[4,3,256]{2,1,0:T(4,128)S(1)}, u32[]{:S(2)}, u32[]{:S(2)}) collective-permute-start(f32[4,3,256]{2,1,0:T(4,128)S(1)} %get-tuple-element.47), channel_id=1, source_target_pairs={{1,0},{2,1},{3,2},{5,4},{6,5},{7,6},{9,8},{10,9},{11,10},{13,12},{... | collective-permute-start | bytes 36872 | tf_op jit(solution)/shard_map/ppermute | solution.py:21
  54.8 3.0 %collective-permute-start.3 = (f32[4,3,256]{2,1,0:T(4,128)S(1)}, f32[4,3,256]{2,1,0:T(4,128)S(1)}, u32[]{:S(2)}, u32[]{:S(2)}) collective-permute-start(f32[4,3,256]{2,1,0:T(4,128)S(1)} %get-tuple-element.46), channel_id=1, source_target_pairs={{0,1},{1,2},{2,3},{4,5},{5,6},{6,7},{8,9},{9,10},{10,11},{12,13},{... | collective-permute-start | bytes 36872 | tf_op jit(solution)/shard_map/ppermute | solution.py:21
  57.9 0.8 collective-permute-done.3
  58.7 4.4 %collective-permute-start.5 = (f32[5,70,256]{2,1,0:T(8,128)S(1)}, f32[5,70,256]{2,1,0:T(8,128)S(1)}, u32[]{:S(2)}, u32[]{:S(2)}) collective-permute-start(f32[5,70,256]{2,1,0:T(8,128)S(1)} %pad_maximum_fusion.2), channel_id=1, source_target_pairs={{0,4},{4,8},{8,12},{1,5},{5,9},{9,13},{2,6},{6,10},{10,14},{3,7},{... | collective-permute-start | bytes 1075208 | tf_op jit(solution)/shard_map/ppermute | solution.py:21
  63.3 8.3 %collective-permute-done.5 = f32[5,70,256]{2,1,0:T(8,128)S(1)} collective-permute-done((f32[5,70,256]{2,1,0:T(8,128)S(1)}, f32[5,70,256]{2,1,0:T(8,128)S(1)}, u32[]{:S(2)}, u32[]{:S(2)}) %collective-permute-start.5) | collective-permute-done | bytes 358432 | tf_op jit(solution)/shard_map/ppermute | solution.py:21
  71.6 0.7 copy-done.3
  73.1 5.4 %collective-permute-start.6 = (f32[2,70,256]{2,1,0:T(8,128)S(1)}, f32[2,70,256]{2,1,0:T(8,128)S(1)}, u32[]{:S(2)}, u32[]{:S(2)}) collective-permute-start(f32[2,70,256]{2,1,0:T(8,128)S(1)} %add.356), channel_id=1, source_target_pairs={{0,8},{4,12},{1,9},{5,13},{2,10},{6,14},{3,11},{7,15},{16,24},{20,... | collective-permute-start | bytes 430088 | tf_op jit(solution)/shard_map/ppermute | solution.py:21
  79.1 3.0 %collective-permute-done.6 = f32[2,70,256]{2,1,0:T(8,128)S(1)} collective-permute-done((f32[2,70,256]{2,1,0:T(8,128)S(1)}, f32[2,70,256]{2,1,0:T(8,128)S(1)}, u32[]{:S(2)}, u32[]{:S(2)}) %collective-permute-start.6) | collective-permute-done | bytes 143392 | tf_op jit(solution)/shard_map/ppermute | solution.py:21
  82.2 5.0 %collective-permute-start.8 = (bf16[2,66,256]{2,1,0:T(8,128)(2,1)S(1)}, bf16[2,66,256]{2,1,0:T(8,128)(2,1)S(1)}, u32[]{:S(2)}, u32[]{:S(2)}) collective-permute-start(bf16[2,66,256]{2,1,0:T(8,128)(2,1)S(1)} %slice.980), channel_id=1, source_target_pairs={{0,4},{4,8},{8,12},{1,5},{5,9},{9,13},{2,6},{6,10},{10,14},{3,7},{... | collective-permute-start | bytes 202760 | tf_op jit(solution)/shard_map/ppermute | solution.py:21
  87.3 1.3 %collective-permute-start.7 = (bf16[2,66,256]{2,1,0:T(8,128)(2,1)S(1)}, bf16[2,66,256]{2,1,0:T(8,128)(2,1)S(1)}, u32[]{:S(2)}, u32[]{:S(2)}) collective-permute-start(bf16[2,66,256]{2,1,0:T(8,128)(2,1)S(1)} %slice.980), channel_id=1, source_target_pairs={{4,0},{8,4},{12,8},{5,1},{9,5},{13,9},{6,2},{10,6},{14,10},{7,3},{... | collective-permute-start | bytes 202760 | tf_op jit(solution)/shard_map/ppermute | solution.py:21
  89.5 4.0 %collective-permute-done.7 = bf16[2,66,256]{2,1,0:T(8,128)(2,1)S(1)} collective-permute-done((bf16[2,66,256]{2,1,0:T(8,128)(2,1)S(1)}, bf16[2,66,256]{2,1,0:T(8,128)(2,1)S(1)}, u32[]{:S(2)}, u32[]{:S(2)}) %collective-permute-start.7) | collective-permute-done | bytes 67616 | tf_op jit(solution)/shard_map/ppermute | solution.py:21
  94.1 4.0 %collective-permute-start.10 = (bf16[2,64,256]{2,1,0:T(8,128)(2,1)S(1)}, bf16[2,64,256]{2,1,0:T(8,128)(2,1)S(1)}, u32[]{:S(2)}, u32[]{:S(2)}) collective-permute-start(bf16[2,64,256]{2,1,0:T(8,128)(2,1)S(1)} %fusion.66), channel_id=1, source_target_pairs={{0,4},{4,8},{8,12},{1,5},{5,9},{9,13},{2,6},{6,10},{10,14},{3,7},{... | collective-permute-start | bytes 196616 | tf_op jit(solution)/shard_map/ppermute | solution.py:21
  98.1 1.3 %collective-permute-start.9 = (bf16[2,64,256]{2,1,0:T(8,128)(2,1)S(1)}, bf16[2,64,256]{2,1,0:T(8,128)(2,1)S(1)}, u32[]{:S(2)}, u32[]{:S(2)}) collective-permute-start(bf16[2,64,256]{2,1,0:T(8,128)(2,1)S(1)} %fusion.66), channel_id=1, source_target_pairs={{4,0},{8,4},{12,8},{5,1},{9,5},{13,9},{6,2},{10,6},{14,10},{7,3},{... | collective-permute-start | bytes 196616 | tf_op jit(solution)/shard_map/ppermute | solution.py:21
  100.0 4.3 %collective-permute-done.9 = bf16[2,64,256]{2,1,0:T(8,128)(2,1)S(1)} collective-permute-done((bf16[2,64,256]{2,1,0:T(8,128)(2,1)S(1)}, bf16[2,64,256]{2,1,0:T(8,128)(2,1)S(1)}, u32[]{:S(2)}, u32[]{:S(2)}) %collective-permute-start.9) | collective-permute-done | bytes 65568 | tf_op jit(solution)/shard_map/ppermute | solution.py:21
  104.6 0.9 fusion.62
  (85 shorter events, 6.3 us)
Async XLA Ops:
  2.9 4.5 %copy-start.1 = (s32[1,64,256]{2,1,0:T(8,128)S(1)}, s32[1,64,256]{2,1,0:T(8,128)}, u32[]{:S(2)}) copy-start(s32[1,64,256]{2,1,0:T(8,128)} %param.8) | copy-start | bytes 196612
  2.9 6.9 %collective-permute-start.1 = (bf16[7,16,256]{2,1,0:T(8,128)(2,1)S(1)}, bf16[7,16,256]{2,1,0:T(8,128)(2,1)S(1)}, u32[]{:S(2)}, u32[]{:S(2)}) collective-permute-start(bf16[7,16,256]{2,1,0:T(8,128)(2,1)S(1)} %pad_maximum_fusion.5), channel_id=1, source_target_pairs={{1,0},{2,1},{3,2},{5,4},{6,5},{7,6},{9,8},{10,9},{11,10},{13,12},{... | collective-permute-start | bytes 172040 | tf_op jit(solution)/shard_map/ppermute | solution.py:21
  4.3 5.5 %collective-permute-start = (bf16[7,16,256]{2,1,0:T(8,128)(2,1)S(1)}, bf16[7,16,256]{2,1,0:T(8,128)(2,1)S(1)}, u32[]{:S(2)}, u32[]{:S(2)}) collective-permute-start(bf16[7,16,256]{2,1,0:T(8,128)(2,1)S(1)} %pad_maximum_fusion.4), channel_id=1, source_target_pairs={{0,1},{1,2},{2,3},{4,5},{5,6},{6,7},{8,9},{9,10},{10,11},{12,13},{... | collective-permute-start | bytes 172040 | tf_op jit(solution)/shard_map/ppermute | solution.py:21
  7.4 0.7 copy-start.2
  8.3 0.7 copy-start.4
  10.0 20.1 %collective-permute-start.2 = (bf16[81,16,256]{2,1,0:T(8,128)(2,1)S(1)}, bf16[81,16,256]{2,1,0:T(8,128)(2,1)S(1)}, u32[]{:S(2)}, u32[]{:S(2)}) collective-permute-start(bf16[81,16,256]{2,1,0:T(8,128)(2,1)S(1)} %pad_maximum_fusion), channel_id=1, source_target_pairs={{4,0},{8,4},{12,8},{5,1},{9,5},{13,9},{6,2},{10,6},{14,10},{7,3},{... | collective-permute-start | bytes 1990664 | tf_op jit(solution)/shard_map/ppermute | solution.py:21
  53.5 4.4 %collective-permute-start.4 = (f32[4,3,256]{2,1,0:T(4,128)S(1)}, f32[4,3,256]{2,1,0:T(4,128)S(1)}, u32[]{:S(2)}, u32[]{:S(2)}) collective-permute-start(f32[4,3,256]{2,1,0:T(4,128)S(1)} %get-tuple-element.47), channel_id=1, source_target_pairs={{1,0},{2,1},{3,2},{5,4},{6,5},{7,6},{9,8},{10,9},{11,10},{13,12},{... | collective-permute-start | bytes 36872 | tf_op jit(solution)/shard_map/ppermute | solution.py:21
  54.8 3.9 %collective-permute-start.3 = (f32[4,3,256]{2,1,0:T(4,128)S(1)}, f32[4,3,256]{2,1,0:T(4,128)S(1)}, u32[]{:S(2)}, u32[]{:S(2)}) collective-permute-start(f32[4,3,256]{2,1,0:T(4,128)S(1)} %get-tuple-element.46), channel_id=1, source_target_pairs={{0,1},{1,2},{2,3},{4,5},{5,6},{6,7},{8,9},{9,10},{10,11},{12,13},{... | collective-permute-start | bytes 36872 | tf_op jit(solution)/shard_map/ppermute | solution.py:21
  58.7 12.9 %collective-permute-start.5 = (f32[5,70,256]{2,1,0:T(8,128)S(1)}, f32[5,70,256]{2,1,0:T(8,128)S(1)}, u32[]{:S(2)}, u32[]{:S(2)}) collective-permute-start(f32[5,70,256]{2,1,0:T(8,128)S(1)} %pad_maximum_fusion.2), channel_id=1, source_target_pairs={{0,4},{4,8},{8,12},{1,5},{5,9},{9,13},{2,6},{6,10},{10,14},{3,7},{... | collective-permute-start | bytes 1075208 | tf_op jit(solution)/shard_map/ppermute | solution.py:21
  71.6 0.7 copy-start.3
  73.1 8.9 %collective-permute-start.6 = (f32[2,70,256]{2,1,0:T(8,128)S(1)}, f32[2,70,256]{2,1,0:T(8,128)S(1)}, u32[]{:S(2)}, u32[]{:S(2)}) collective-permute-start(f32[2,70,256]{2,1,0:T(8,128)S(1)} %add.356), channel_id=1, source_target_pairs={{0,8},{4,12},{1,9},{5,13},{2,10},{6,14},{3,11},{7,15},{16,24},{20,... | collective-permute-start | bytes 430088 | tf_op jit(solution)/shard_map/ppermute | solution.py:21
  82.2 7.0 %collective-permute-start.8 = (bf16[2,66,256]{2,1,0:T(8,128)(2,1)S(1)}, bf16[2,66,256]{2,1,0:T(8,128)(2,1)S(1)}, u32[]{:S(2)}, u32[]{:S(2)}) collective-permute-start(bf16[2,66,256]{2,1,0:T(8,128)(2,1)S(1)} %slice.980), channel_id=1, source_target_pairs={{0,4},{4,8},{8,12},{1,5},{5,9},{9,13},{2,6},{6,10},{10,14},{3,7},{... | collective-permute-start | bytes 202760 | tf_op jit(solution)/shard_map/ppermute | solution.py:21
  87.3 6.2 %collective-permute-start.7 = (bf16[2,66,256]{2,1,0:T(8,128)(2,1)S(1)}, bf16[2,66,256]{2,1,0:T(8,128)(2,1)S(1)}, u32[]{:S(2)}, u32[]{:S(2)}) collective-permute-start(bf16[2,66,256]{2,1,0:T(8,128)(2,1)S(1)} %slice.980), channel_id=1, source_target_pairs={{4,0},{8,4},{12,8},{5,1},{9,5},{13,9},{6,2},{10,6},{14,10},{7,3},{... | collective-permute-start | bytes 202760 | tf_op jit(solution)/shard_map/ppermute | solution.py:21
  94.1 10.2 %copy-start = (f32[2,64,256]{2,1,0:T(8,128)S(1)}, f32[2,64,256]{2,1,0:T(8,128)}, u32[]{:S(2)}) copy-start(f32[2,64,256]{2,1,0:T(8,128)} %get-tuple-element.16) | copy-start | bytes 393220
  94.1 5.9 %collective-permute-start.10 = (bf16[2,64,256]{2,1,0:T(8,128)(2,1)S(1)}, bf16[2,64,256]{2,1,0:T(8,128)(2,1)S(1)}, u32[]{:S(2)}, u32[]{:S(2)}) collective-permute-start(bf16[2,64,256]{2,1,0:T(8,128)(2,1)S(1)} %fusion.66), channel_id=1, source_target_pairs={{0,4},{4,8},{8,12},{1,5},{5,9},{9,13},{2,6},{6,10},{10,14},{3,7},{... | collective-permute-start | bytes 196616 | tf_op jit(solution)/shard_map/ppermute | solution.py:21
  98.1 6.2 %collective-permute-start.9 = (bf16[2,64,256]{2,1,0:T(8,128)(2,1)S(1)}, bf16[2,64,256]{2,1,0:T(8,128)(2,1)S(1)}, u32[]{:S(2)}, u32[]{:S(2)}) collective-permute-start(bf16[2,64,256]{2,1,0:T(8,128)(2,1)S(1)} %fusion.66), channel_id=1, source_target_pairs={{4,0},{8,4},{12,8},{5,1},{9,5},{13,9},{6,2},{10,6},{14,10},{7,3},{... | collective-permute-start | bytes 196616 | tf_op jit(solution)/shard_map/ppermute | solution.py:21

commit v3 on v2

--- a/solution.py
+++ b/solution.py
@@ -15,10 +15,9 @@
 tile_axes = ("xy", "col")
 
 
-def shifted(value, axis, steps):
+def ringed(value, axis, steps):
     count = lax.axis_size(axis)
-    initial, last = (max(0, -steps), min(count, count - steps))
-    return lax.ppermute(value, axis, [(source, source + steps) for source in range(initial, last)])
+    return lax.ppermute(value, axis, [(i, (i + steps) % count) for i in range(count)])
 
 
 BLOCK = 4
@@ -28,12 +27,15 @@
 MASKED = -1e30
 
 
-def flow_kernel(e_ref, l_ref, f_ref, b_ref, t_ref, bias_ref, o_ref, s0_ref, s1_ref, s2_ref, s3_ref, w_ref):
-
-    rows = f_ref.shape[1]
-    channels, breadth = e_ref.shape[1], e_ref.shape[2]
-    groups = rows // GROUP
-    steps = breadth // BLOCK // (2 // groups)
+def flow_kernel(
+    early_rows, late_rows, n_early, live_ref, *refs
+):
+    n_in = n_early + 1 + max(i for i, _ in late_rows)
+    ins, out_ref = refs[:n_in], refs[n_in]
+    t_ref, bias_ref, o_ref, s0_ref, s1_ref, s2_ref, s3_ref, w_ref = refs[n_in + 1 :]
+    channels, breadth = ins[0].shape[1:]
+    groups = 1
+    steps = breadth // BLOCK // 2
     wide = t_ref.shape[3]
     lane = lax.broadcasted_iota(jnp.int32, (8, 128), 1)
     sub = lax.broadcasted_iota(jnp.int32, (8, 128), 0)
@@ -55,12 +57,14 @@
         0.0,
     ).astype(jnp.bfloat16)
     per = GROUP // BLOCK
-    for side, ref in enumerate((e_ref, l_ref)):
+    for side, (offset, table) in enumerate(((0, early_rows), (n_early, late_rows))):
         for g in range(groups):
             for kr in range(0, SPAN, 2):
-                pieces = [
-                    ref[GROUP * g + kr + k + BLOCK * b] for k in range(2) for b in range(per)
-                ]
+                pieces = []
+                for k in range(2):
+                    for b in range(per):
+                        which, row = table[SPAN * b + kr + k]
+                        pieces.append(ins[offset + which][row])
                 flat = jnp.concatenate(pieces, axis=0)
                 out = lax.dot_general(
                     place, flat, (((1,), (1,)), ((), ())), preferred_element_type=jnp.float32
@@ -75,8 +79,8 @@
         def tiles_of(i):
             tiles = []
             for k in range(2):
-                g = k if groups == 2 else 0
-                base = i * BLOCK + (0 if groups == 2 else k * (breadth // 2))
+                g = 0
+                base = i * BLOCK + k * (breadth // 2)
                 tiles.append((g, base))
             return tiles
 
@@ -173,44 +177,45 @@
         score(0, s0_ref)
         score(1, s1_ref)
         lax.fori_loop(0, steps // 4, step, 0)
-    for side, ref in enumerate((f_ref, b_ref)):
+    live = live_ref[0]
+    for side in range(2):
         for comp in range(2):
-            for g in range(groups):
-                turned = jnp.transpose(o_ref[side, comp, g], (1, 0))
-                for t in range(breadth // 128):
-                    for r in range(BLOCK):
-                        w_ref[side, comp, g, t, pl.ds(r, per, stride=BLOCK), :] = turned[
-                            per * r : per * r + per, 128 * t : 128 * t + 128
-                        ]
-                    ref[comp, GROUP * g : GROUP * g + GROUP, 128 * t : 128 * t + 128] = w_ref[
-                        side, comp, g, t
+            turned = jnp.transpose(o_ref[side, comp, 0], (1, 0)) * live
+            for t in range(breadth // 128):
+                for r in range(BLOCK):
+                    w_ref[side, comp, t, pl.ds(r, per, stride=BLOCK), :] = turned[
+                        per * r : per * r + per, 128 * t : 128 * t + 128
                     ]
-
-
-def flows(early, late):
-    rows = early.shape[0] - 2 * RADIUS
-    channels, breadth = early.shape[1:]
-    groups = rows // GROUP
+                out_ref[2 * side + comp, :, 128 * t : 128 * t + 128] = w_ref[side, comp, t]
+
+
+def flows(live, early, late, early_at, late_at, starts):
+    channels, breadth = early[0].shape[1:]
     wide = breadth + 16
-    out = jax.ShapeDtypeStruct((2, rows, breadth), jnp.float32)
+    tables = [
+        [at(start - RADIUS + k) for start in starts for k in range(SPAN)]
+        for at in (early_at, late_at)
+    ]
+    cells = GROUP * breadth
     return pl.pallas_call(
-        flow_kernel,
-        out_shape=(out, out),
-        in_specs=[pl.BlockSpec(memory_space=pltpu.VMEM)] * 2,
-        out_specs=(pl.BlockSpec(memory_space=pltpu.VMEM),) * 2,
+        functools.partial(flow_kernel, *tables, len(early)),
+        out_shape=jax.ShapeDtypeStruct((4, GROUP, breadth), jnp.float32),
+        in_specs=[pl.BlockSpec(memory_space=pltpu.SMEM)]
+        + [pl.BlockSpec(memory_space=pltpu.VMEM)] * (len(early) + len(late)),
+        out_specs=pl.BlockSpec(memory_space=pltpu.VMEM),
         scratch_shapes=[
-            pltpu.VMEM((2, groups, SPAN, wide, 128), jnp.float32),
+            pltpu.VMEM((2, 1, SPAN, wide, 128), jnp.float32),
             pltpu.VMEM((12, 8, 128), jnp.float32),
-            pltpu.VMEM((2, 2, groups, breadth, 128), jnp.float32),
-            pltpu.VMEM((SPAN * SPAN, 256), jnp.float32),
-            pltpu.VMEM((SPAN * SPAN, 256), jnp.float32),
-            pltpu.VMEM((SPAN * SPAN, 256), jnp.float32),
-            pltpu.VMEM((SPAN * SPAN, 256), jnp.float32),
-            pltpu.VMEM((2, 2, groups, breadth // 128, GROUP, 128), jnp.float32),
-        ],
-        compiler_params=pltpu.CompilerParams(vmem_limit_bytes=40 * 2**20),
+            pltpu.VMEM((2, 2, 1, breadth, 128), jnp.float32),
+        ]
+        + [pltpu.VMEM((SPAN * SPAN, 256), jnp.float32)] * 4
+        + [pltpu.VMEM((2, 2, breadth // 128, GROUP, 128), jnp.float32)],
+        compiler_params=pltpu.CompilerParams(vmem_limit_bytes=24 * 2**20),
+        cost_estimate=pl.CostEstimate(
+            flops=2 * cells * SPAN * SPAN * 2 * 256, bytes_accessed=2**22, transcendentals=2 * cells * SPAN * SPAN
+        ),
         name="flows",
-    )(early, late)
+    )(live, *early, *late)
 
 
 def spring(vector):
@@ -242,54 +247,86 @@
     return step_size * (pulls + below * (spring(down - backward) - spring(-down - prior)))
 
 
-def prefix(pair_sum):
+def prefix(pair_sum, section):
     count = lax.axis_size("gz")
+
+    def earlier(value, steps):
+        return jnp.where(section >= steps, ringed(value, "gz", steps), 0.0)
+
     reach = 2
     while reach < count - 2:
-        pair_sum = pair_sum + shifted(pair_sum, "gz", reach)
+        pair_sum = pair_sum + earlier(pair_sum, reach)
         reach *= 2
-    return shifted(pair_sum, "gz", 2)
+    return earlier(pair_sum, 2)
 
 
 def on_device(features, class_map, stiffness, valid):
     center = jnp.transpose(features[0], (1, 0, 2))
     height, channels, breadth = center.shape
+    section, sections = lax.axis_index("gz"), lax.axis_size("gz")
+    tile, tiles = lax.axis_index(tile_axes), lax.axis_size(tile_axes)
+    quarter = height // 4
+    low, high = quarter - RADIUS, height - quarter + RADIUS
+
+    upper_mid = ringed(center[low:high], "gz", -1)
+
     codes = (class_map[0] + 1).astype(jnp.bfloat16).reshape(-1, channels, breadth)
-    section = lax.axis_index("gz")
-    tile = lax.axis_index(tile_axes)
-
     top = jnp.concatenate([center[:RADIUS], codes[:1]])
     bottom = jnp.concatenate([center[-RADIUS:], codes[-1:]])
-    before = shifted(bottom, tile_axes, 1)
-    after = shifted(top, tile_axes, -1)
-    padded = jnp.concatenate([before[:RADIUS], center, after[:RADIUS]])
+    nothing = jnp.zeros_like(top)
+    before = jnp.where(tile > 0, ringed(bottom, tile_axes, 1), nothing)
+    after = jnp.where(tile < tiles - 1, ringed(top, tile_axes, -1), nothing)
     own_codes = jnp.concatenate(
-        [
-            before[RADIUS, -STEPS:],
-            codes.reshape(height, breadth),
-            after[RADIUS, :STEPS],
-        ]
+        [before[RADIUS, -STEPS:], codes.reshape(height, breadth), after[RADIUS, :STEPS]]
     )
     spare = -own_codes.shape[0] % channels
     packed = jnp.pad(own_codes, ((0, spare), (0, 0))).reshape(-1, channels, breadth)
-    upper = shifted(jnp.concatenate([padded, packed]), "gz", -1)
-    upper_pad = upper[: padded.shape[0]]
-    upper_codes = upper[padded.shape[0] :].reshape(-1, breadth)[: own_codes.shape[0]]
-    forward, ahead = flows(padded, upper_pad)
-
-    both = jnp.concatenate([forward, ahead])
-    both = jnp.concatenate(
+    upper_out = ringed(
+        jnp.concatenate([before[:RADIUS], center[:low], center[high:], after[:RADIUS], packed]),
+        "gz",
+        -1,
+    )
+    outer = low + RADIUS
+    upper_codes = upper_out[2 * outer :].reshape(-1, breadth)[: own_codes.shape[0]]
+
+    def own_at(row):
+        if row < 0:
+            return 1, row + RADIUS
+        return (0, row) if row < height else (2, row - height)
+
+    def upper_at(row):
+        if low <= row < high:
+            return 0, row - low
+        return (1, row + RADIUS) if row < low else (1, row - high + outer)
+
+    live = jnp.where(section < sections - 1, 1.0, 0.0)[None]
+    middle_rows = range(quarter, height - quarter, BLOCK)
+    middle = flows(live, [center], [upper_mid], own_at, upper_at, middle_rows)
+    lower_mid = ringed(
+        jnp.concatenate([middle.reshape(-1, breadth), own_codes.astype(jnp.float32)]), "gz", 1
+    )
+    outer_rows = [*range(0, quarter, BLOCK), *range(height - quarter, height, BLOCK)]
+    outside = flows(
+        live, [center, before, after], [upper_mid, upper_out], own_at, upper_at, outer_rows
+    )
+
+    head, tail = outside[:, :quarter], outside[:, quarter:]
+    head = jnp.concatenate([ringed(tail[:, -STEPS:], tile_axes, 1), head], axis=1)
+    tail = jnp.concatenate([tail, ringed(outside[:, :STEPS], tile_axes, -1)], axis=1)
+    lower_out = ringed(jnp.concatenate([head, tail], axis=1), "gz", 1)
+    both = jnp.concatenate([head, middle, tail], axis=1)
+    n_mid = middle.shape[0] * middle.shape[1]
+    lower = jnp.concatenate(
         [
-            shifted(both[:, -STEPS:], tile_axes, 1),
-            both,
-            shifted(both[:, :STEPS], tile_axes, -1),
+            lower_out[:, : head.shape[1]],
+            lower_mid[:n_mid].reshape(middle.shape),
+            lower_out[:, head.shape[1] :],
         ],
         axis=1,
     )
-    message = jnp.concatenate([both, own_codes[None].astype(jnp.float32)])
-    lower = shifted(message, "gz", 1)
     fwd, ahd = both[:2], both[2:]
-    pri, bwd = lower[:2], lower[2:4]
+    pri, bwd = lower[:2], lower[2:]
+    forward = fwd[:, STEPS:-STEPS]
 
     def stiff_of(code):
         levels = jnp.arange(stiffness.shape[0], dtype=jnp.float32)[:, None, None] + 1.0
@@ -299,23 +336,27 @@
 
     stiff, inside = stiff_of(own_codes)
     stiff_up, inside_up = stiff_of(upper_codes)
-    stiff_down, inside_down = stiff_of(lower[4])
+    stiff_down, inside_down = stiff_of(lower_mid[n_mid:])
 
     sound = jnp.pad(valid.astype(jnp.float32), ((1, 1), (1, 1)))
     near = lax.dynamic_slice(sound, (section, tile), (3, 3))
     links = near[:-1] * near[1:]
-    by_row = jnp.repeat(
-        links, jnp.array([STEPS, height, STEPS]), axis=1, total_repeat_length=height + 2 * STEPS
+    by_row = jnp.concatenate(
+        [
+            jnp.broadcast_to(links[:, k : k + 1], (2, count))
+            for k, count in enumerate((STEPS, height, STEPS))
+        ],
+        axis=1,
     )
     below, here = by_row[0][None, :, None], by_row[1][None, :, None]
 
     gain = here * (fwd - ahd)
     gain_below = below * (pri - bwd)
-    start = 0.5 * (prefix(gain + gain_below) + gain_below)
+    start = 0.5 * (prefix(gain + gain_below, section) + gain_below)
     pull = force(0.5 * gain, -0.5 * gain_below, here, below, fwd, ahd, pri, bwd)
     sent = trim(2, pull).astype(jnp.bfloat16)
-    pull_up = shifted(sent, "gz", -1).astype(jnp.float32)
-    pull_down = shifted(sent, "gz", 1).astype(jnp.float32)
+    pull_up = ringed(sent, "gz", -1).astype(jnp.float32)
+    pull_down = ringed(sent, "gz", 1).astype(jnp.float32)
 
     start_up = start + 0.5 * gain
     start_down = start - 0.5 * gain_below
@@ -331,8 +372,8 @@
     )
     change = trim(1, second) - trim(3, start)
     change = change.astype(jnp.bfloat16)
-    last_up = trim(3, start_up) + shifted(change, "gz", -1).astype(jnp.float32)
-    last_down = trim(3, start_down) + shifted(change, "gz", 1).astype(jnp.float32)
+    last_up = trim(3, start_up) + ringed(change, "gz", -1).astype(jnp.float32)
+    last_down = trim(3, start_down) + ringed(change, "gz", 1).astype(jnp.float32)
     fields = [trim(1, x) for x in fields]
     mid = trim(1, second)
     third = relaxed(second, trim(2, stiff), trim(2, inside)) + force(

time: 106 us -> 83.4 us (0.79)
  waiting for transfers between devices: 39.7 us -> 29.4 us
  starting transfers between devices: 31.4 us -> 21.3 us
  local copies, waits for them, and re-layouts: 5.51 us -> 4.05 us
    ppermute x11 -> x13, waiting for transfers between devices: 39.7 us -> 29.4 us  [ringed(): lax.ppermute(value, axis, [(i, (i + steps) % count) for i in range(count)])]
    ppermute x11 -> x13, starting transfers between devices: 31.4 us -> 21.3 us  [ringed(): lax.ppermute(value, axis, [(i, (i + steps) % count) for i in range(count)])]
    unnamed x13 -> x11, local copies, waits for them, and re-layouts: 4.27 us -> 2.7 us
    pallas_call x1 -> x2, Pallas kernels: 22.4 us -> 22.5 us  [flows(): pl.pallas_call(functools.partial(flow_kernel, *tables, len(early)), out_s...]
  transfers between devices with their start and end apart: 11 -> 13, of which waited for: 8 -> 7; matrix products, arithmetic and copies ran while one was open for 3% -> 3% of each run, Pallas kernels for 0% -> 27%
where the time goes in v3:
time: 83.4 us; the launch traced here: 83.2 us
  waiting for transfers between devices  29.4 us (35%)
  Pallas kernels  22.5 us (27%)
  starting transfers between devices  21.3 us (26%)
  other arithmetic  4.79 us (6%)
  local copies, waits for them, and re-layouts  4.05 us (5%)
  between operations  1.17 us (1%)
    ppermute x13, waiting for transfers between devices, ringed(): lax.ppermute(value, axis, [(i, (i + steps) % count) for i in range(count)])  29.4 us
    pallas_call x2, Pallas kernels, flows(): pl.pallas_call(functools.partial(flow_kernel, *tables, len(early)), out_s...  22.5 us
    ppermute x13, starting transfers between devices, ringed(): lax.ppermute(value, axis, [(i, (i + steps) % count) for i in range(count)])  21.3 us
    unnamed x11, local copies, waits for them, and re-layouts  2.7 us
  transfers between devices with their start and end apart: 13, of which 7 were waited for; matrix products, arithmetic and copies ran while one was open for 3% of the time, Pallas kernels for 27%

profile of v3, /device:TPU:0, one launch (start us, length us, event | category | flops | bytes accessed | tf_op | source)
XLA Modules:
  0.0 83.2 jit_solution(11994297038343368064)
XLA Ops:
  0.6 1.4 %copy.9 = bf16[1,16,64,256]{3,1,2,0:T(8,128)(2,1)S(1)} copy(bf16[1,16,64,256]{3,2,1,0:T(8,128)(2,1)} %param.4) | data formatting | bytes 1048576 | tf_op args[0]
  2.1 0.5 collective-permute-start
  2.6 2.0 %collective-permute-start.1 = (bf16[7,16,256]{2,1,0:T(8,128)(2,1)S(1)}, bf16[7,16,256]{2,1,0:T(8,128)(2,1)S(1)}, u32[]{:S(2)}, u32[]{:S(2)}) collective-permute-start(bf16[7,16,256]{2,1,0:T(8,128)(2,1)S(1)} %pad_maximum_fusion.5), channel_id=1, source_target_pairs={{0,3},{1,0},{2,1},{3,2},{4,7},{5,4},{6,5},{7,6},{8,11},{9,8},{10,9... | collective-permute-start | bytes 172040 | tf_op jit(solution)/shard_map/ppermute | solution.py:20
  4.6 4.4 %collective-permute-start.2 = (bf16[44,16,256]{2,1,0:T(8,128)(2,1)S(1)}, bf16[44,16,256]{2,1,0:T(8,128)(2,1)S(1)}, u32[]{:S(2)}, u32[]{:S(2)}) collective-permute-start(bf16[44,16,256]{2,1,0:T(8,128)(2,1)S(1)} %slice.506), channel_id=1, source_target_pairs={{0,12},{4,0},{8,4},{12,8},{1,13},{5,1},{9,5},{13,9},{2,14},{6,2},{... | collective-permute-start | bytes 1081352 | tf_op jit(solution)/shard_map/ppermute | solution.py:20
  9.1 0.7 copy-done.1
  10.8 0.5 collective-permute-start.3
  11.3 6.6 %collective-permute-done.2.refs_3_.refs_1_ = bf16[44,16,256]{2,1,0:T(8,128)(2,1)S(1)} collective-permute-done((bf16[44,16,256]{2,1,0:T(8,128)(2,1)S(1)}, bf16[44,16,256]{2,1,0:T(8,128)(2,1)S(1)}, u32[]{:S(2)}, u32[]{:S(2)}) %collective-permute-start.2) | collective-permute-done | bytes 360480 | tf_op jit(solution)/shard_map/ppermute | solution.py:20
  17.9 11.3 %flows.3 = f32[4,32,256]{2,1,0:T(8,128)S(1)} custom-call(f32[1]{0:T(128)} %bitcast.7.live_ref, bf16[64,16,256]{2,1,0:T(8,128)(2,1)S(1)} %bitcast.135, bf16[44,16,256]{2,1,0:T(8,128)(2,1)S(1)} %collective-permute-done.2.refs_3_.refs_1_), custom_call_target="tpu_custom_call" | custom-call | flops 2147483648 | bytes 4194304 | tf_op jit(solution)/shard_map/flows/pallas_call | solution.py:200
  29.7 11.3 %flows.2 = f32[4,32,256]{2,1,0:T(8,128)S(1)} custom-call(f32[1]{0:T(128)} %bitcast.7.live_ref, bf16[64,16,256]{2,1,0:T(8,128)(2,1)S(1)} %bitcast.136, bf16[7,16,256]{2,1,0:T(8,128)(2,1)S(1)} %broadcast_select_fusion.1.refs_1_, bf16[7,16,256]{2,1,0:T(8,128)(2,1)S(1)} %broadcast_select_fusion.refs_2_, ...), custom_call_target="tpu_custom_call" | custom-call | flops 2147483648 | bytes 4194304 | tf_op jit(solution)/shard_map/flows/pallas_call | solution.py:200
  41.1 1.7 %collective-permute-start.5 = (f32[4,3,256]{2,1,0:T(4,128)S(1)}, f32[4,3,256]{2,1,0:T(4,128)S(1)}, u32[]{:S(2)}, u32[]{:S(2)}) collective-permute-start(f32[4,3,256]{2,1,0:T(4,128)S(1)} %get-tuple-element.57), channel_id=1, source_target_pairs={{0,3},{1,0},{2,1},{3,2},{4,7},{5,4},{6,5},{7,6},{8,11},{9,8},{10,9... | collective-permute-start | bytes 36872 | tf_op jit(solution)/shard_map/ppermute | solution.py:20
  42.9 1.3 %collective-permute-done.4 = f32[4,3,256]{2,1,0:T(4,128)S(1)} collective-permute-done((f32[4,3,256]{2,1,0:T(4,128)S(1)}, f32[4,3,256]{2,1,0:T(4,128)S(1)}, u32[]{:S(2)}, u32[]{:S(2)}) %collective-permute-start.4) | collective-permute-done | bytes 12320 | tf_op jit(solution)/shard_map/ppermute | solution.py:20
  44.3 1.6 %collective-permute-start.6 = (f32[4,38,256]{2,1,0:T(8,128)S(1)}, f32[4,38,256]{2,1,0:T(8,128)S(1)}, u32[]{:S(2)}, u32[]{:S(2)}) collective-permute-start(f32[4,38,256]{2,1,0:T(8,128)S(1)} %pad_maximum_fusion.3), channel_id=1, source_target_pairs={{0,4},{4,8},{8,12},{12,0},{1,5},{5,9},{9,13},{13,1},{2,6},{6,10},{... | collective-permute-start | bytes 466952 | tf_op jit(solution)/shard_map/ppermute | solution.py:20
  46.6 5.8 %collective-permute-done.6 = f32[4,38,256]{2,1,0:T(8,128)S(1)} collective-permute-done((f32[4,38,256]{2,1,0:T(8,128)S(1)}, f32[4,38,256]{2,1,0:T(8,128)S(1)}, u32[]{:S(2)}, u32[]{:S(2)}) %collective-permute-start.6) | collective-permute-done | bytes 155680 | tf_op jit(solution)/shard_map/ppermute | solution.py:20
  52.4 0.6 copy-done.2
  53.0 0.7 select_reduce_fusion.1
  53.9 2.9 %collective-permute-start.8 = (f32[2,70,256]{2,1,0:T(8,128)S(1)}, f32[2,70,256]{2,1,0:T(8,128)S(1)}, u32[]{:S(2)}, u32[]{:S(2)}) collective-permute-start(f32[2,70,256]{2,1,0:T(8,128)S(1)} %add.300), channel_id=1, source_target_pairs={{0,8},{4,12},{8,0},{12,4},{1,9},{5,13},{9,1},{13,5},{2,10},{6,14},... | collective-permute-start | bytes 430088 | tf_op jit(solution)/shard_map/ppermute | solution.py:20
  57.4 7.1 %collective-permute-done.8 = f32[2,70,256]{2,1,0:T(8,128)S(1)} collective-permute-done((f32[2,70,256]{2,1,0:T(8,128)S(1)}, f32[2,70,256]{2,1,0:T(8,128)S(1)}, u32[]{:S(2)}, u32[]{:S(2)}) %collective-permute-start.8) | collective-permute-done | bytes 143392 | tf_op jit(solution)/shard_map/ppermute | solution.py:20
  64.7 3.8 %collective-permute-start.9 = (bf16[2,66,256]{2,1,0:T(8,128)(2,1)S(1)}, bf16[2,66,256]{2,1,0:T(8,128)(2,1)S(1)}, u32[]{:S(2)}, u32[]{:S(2)}) collective-permute-start(bf16[2,66,256]{2,1,0:T(8,128)(2,1)S(1)} %slice.1035), channel_id=1, source_target_pairs={{0,12},{4,0},{8,4},{12,8},{1,13},{5,1},{9,5},{13,9},{2,14},{6,2},{... | collective-permute-start | bytes 202760 | tf_op jit(solution)/shard_map/ppermute | solution.py:20
  68.8 2.6 %collective-permute-done.10 = bf16[2,66,256]{2,1,0:T(8,128)(2,1)S(1)} collective-permute-done((bf16[2,66,256]{2,1,0:T(8,128)(2,1)S(1)}, bf16[2,66,256]{2,1,0:T(8,128)(2,1)S(1)}, u32[]{:S(2)}, u32[]{:S(2)}) %collective-permute-start.10) | collective-permute-done | bytes 67616 | tf_op jit(solution)/shard_map/ppermute | solution.py:20
  72.3 3.1 %collective-permute-start.11 = (bf16[2,64,256]{2,1,0:T(8,128)(2,1)S(1)}, bf16[2,64,256]{2,1,0:T(8,128)(2,1)S(1)}, u32[]{:S(2)}, u32[]{:S(2)}) collective-permute-start(bf16[2,64,256]{2,1,0:T(8,128)(2,1)S(1)} %fusion.66), channel_id=1, source_target_pairs={{0,12},{4,0},{8,4},{12,8},{1,13},{5,1},{9,5},{13,9},{2,14},{6,2},{... | collective-permute-start | bytes 196616 | tf_op jit(solution)/shard_map/ppermute | solution.py:20
  75.5 1.8 %collective-permute-done.11 = bf16[2,64,256]{2,1,0:T(8,128)(2,1)S(1)} collective-permute-done((bf16[2,64,256]{2,1,0:T(8,128)(2,1)S(1)}, bf16[2,64,256]{2,1,0:T(8,128)(2,1)S(1)}, u32[]{:S(2)}, u32[]{:S(2)}) %collective-permute-start.11) | collective-permute-done | bytes 65568 | tf_op jit(solution)/shard_map/ppermute | solution.py:20
  77.3 4.2 %collective-permute-done.12 = bf16[2,64,256]{2,1,0:T(8,128)(2,1)S(1)} collective-permute-done((bf16[2,64,256]{2,1,0:T(8,128)(2,1)S(1)}, bf16[2,64,256]{2,1,0:T(8,128)(2,1)S(1)}, u32[]{:S(2)}, u32[]{:S(2)}) %collective-permute-start.12) | collective-permute-done | bytes 65568 | tf_op jit(solution)/shard_map/ppermute | solution.py:20
  81.4 0.8 multiply_reduce_fusion.11
  82.3 0.9 %fusion.62 = f32[1,2,64,256]{3,2,1,0:T(8,128)} fusion(f32[2,66,256]{2,1,0:T(8,128)S(1)} %fusion.17, f32[64,256]{1,0:T(8,128)S(1)} %add_sqrt_fusion.8, f32[64,256]{1,0:T(8,128)S(1)} %add_sqrt_fusion.9, f32[64]{0:T(128)S(1)} %get-tuple-element.69, f32[64,256]{1,0:T(8,128)S(1)} %add_sqrt_fusion.10, f32[64,256]{1,0:T(8,128)S(1)} %add_sqrt_fusion.11, ...), kind=kLoop, calls=%fused_computation.110 | loop fusion | flops 1015808 | bytes 1999872 | tf_op jit(solution)/shard_map/broadcast_in_dim | solution.py:382
  (93 shorter events, 4.6 us)
Async XLA Ops:
  0.6 1.4 %copy-start = (s32[1,64,256]{2,1,0:T(8,128)S(1)}, s32[1,64,256]{2,1,0:T(8,128)}, u32[]{:S(2)}) copy-start(s32[1,64,256]{2,1,0:T(8,128)} %param.5) | copy-start | bytes 196612
  2.1 8.5 %collective-permute-start = (bf16[7,16,256]{2,1,0:T(8,128)(2,1)S(1)}, bf16[7,16,256]{2,1,0:T(8,128)(2,1)S(1)}, u32[]{:S(2)}, u32[]{:S(2)}) collective-permute-start(bf16[7,16,256]{2,1,0:T(8,128)(2,1)S(1)} %pad_maximum_fusion.4), channel_id=1, source_target_pairs={{0,1},{1,2},{2,3},{3,0},{4,5},{5,6},{6,7},{7,4},{8,9},{9,10},{10,1... | collective-permute-start | bytes 172040 | tf_op jit(solution)/shard_map/ppermute | solution.py:20
  2.6 8.0 %collective-permute-start.1 = (bf16[7,16,256]{2,1,0:T(8,128)(2,1)S(1)}, bf16[7,16,256]{2,1,0:T(8,128)(2,1)S(1)}, u32[]{:S(2)}, u32[]{:S(2)}) collective-permute-start(bf16[7,16,256]{2,1,0:T(8,128)(2,1)S(1)} %pad_maximum_fusion.5), channel_id=1, source_target_pairs={{0,3},{1,0},{2,1},{3,2},{4,7},{5,4},{6,5},{7,6},{8,11},{9,8},{10,9... | collective-permute-start | bytes 172040 | tf_op jit(solution)/shard_map/ppermute | solution.py:20
  4.6 13.2 %collective-permute-start.2 = (bf16[44,16,256]{2,1,0:T(8,128)(2,1)S(1)}, bf16[44,16,256]{2,1,0:T(8,128)(2,1)S(1)}, u32[]{:S(2)}, u32[]{:S(2)}) collective-permute-start(bf16[44,16,256]{2,1,0:T(8,128)(2,1)S(1)} %slice.506), channel_id=1, source_target_pairs={{0,12},{4,0},{8,4},{12,8},{1,13},{5,1},{9,5},{13,9},{2,14},{6,2},{... | collective-permute-start | bytes 1081352 | tf_op jit(solution)/shard_map/ppermute | solution.py:20
  9.1 0.7 copy-start.1
  10.8 18.9 %collective-permute-start.3 = (bf16[37,16,256]{2,1,0:T(8,128)(2,1)S(1)}, bf16[37,16,256]{2,1,0:T(8,128)(2,1)S(1)}, u32[]{:S(2)}, u32[]{:S(2)}) collective-permute-start(bf16[37,16,256]{2,1,0:T(8,128)(2,1)S(1)} %constant_dynamic-update-slice_fusion), channel_id=1, source_target_pairs={{0,12},{4,0},{8,4},{12,8},{1,13},{5,1},{9,5},{13,9},{2,14},{6,2},{... | collective-permute-start | bytes 909320 | tf_op jit(solution)/shard_map/ppermute | solution.py:20
  29.2 23.2 %collective-permute-start.7 = (f32[198,256]{1,0:T(8,128)S(1)}, f32[198,256]{1,0:T(8,128)S(1)}, u32[]{:S(2)}, u32[]{:S(2)}) collective-permute-start(f32[198,256]{1,0:T(8,128)S(1)} %pad_maximum_fusion.2), channel_id=1, source_target_pairs={{0,4},{4,8},{8,12},{12,0},{1,5},{5,9},{9,13},{13,1},{2,6},{6,10},{... | collective-permute-start | bytes 608264 | tf_op jit(solution)/shard_map/ppermute | solution.py:20
  41.0 3.2 %collective-permute-start.4 = (f32[4,3,256]{2,1,0:T(4,128)S(1)}, f32[4,3,256]{2,1,0:T(4,128)S(1)}, u32[]{:S(2)}, u32[]{:S(2)}) collective-permute-start(f32[4,3,256]{2,1,0:T(4,128)S(1)} %get-tuple-element.58), channel_id=1, source_target_pairs={{0,1},{1,2},{2,3},{3,0},{4,5},{5,6},{6,7},{7,4},{8,9},{9,10},{10,1... | collective-permute-start | bytes 36872 | tf_op jit(solution)/shard_map/ppermute | solution.py:20
  41.1 3.2 %collective-permute-start.5 = (f32[4,3,256]{2,1,0:T(4,128)S(1)}, f32[4,3,256]{2,1,0:T(4,128)S(1)}, u32[]{:S(2)}, u32[]{:S(2)}) collective-permute-start(f32[4,3,256]{2,1,0:T(4,128)S(1)} %get-tuple-element.57), channel_id=1, source_target_pairs={{0,3},{1,0},{2,1},{3,2},{4,7},{5,4},{6,5},{7,6},{8,11},{9,8},{10,9... | collective-permute-start | bytes 36872 | tf_op jit(solution)/shard_map/ppermute | solution.py:20
  44.3 8.1 %collective-permute-start.6 = (f32[4,38,256]{2,1,0:T(8,128)S(1)}, f32[4,38,256]{2,1,0:T(8,128)S(1)}, u32[]{:S(2)}, u32[]{:S(2)}) collective-permute-start(f32[4,38,256]{2,1,0:T(8,128)S(1)} %pad_maximum_fusion.3), channel_id=1, source_target_pairs={{0,4},{4,8},{8,12},{12,0},{1,5},{5,9},{9,13},{13,1},{2,6},{6,10},{... | collective-permute-start | bytes 466952 | tf_op jit(solution)/shard_map/ppermute | solution.py:20
  52.4 0.7 copy-start.2
  53.9 10.6 %collective-permute-start.8 = (f32[2,70,256]{2,1,0:T(8,128)S(1)}, f32[2,70,256]{2,1,0:T(8,128)S(1)}, u32[]{:S(2)}, u32[]{:S(2)}) collective-permute-start(f32[2,70,256]{2,1,0:T(8,128)S(1)} %add.300), channel_id=1, source_target_pairs={{0,8},{4,12},{8,0},{12,4},{1,9},{5,13},{9,1},{13,5},{2,10},{6,14},... | collective-permute-start | bytes 430088 | tf_op jit(solution)/shard_map/ppermute | solution.py:20
  64.7 6.7 %collective-permute-start.10 = (bf16[2,66,256]{2,1,0:T(8,128)(2,1)S(1)}, bf16[2,66,256]{2,1,0:T(8,128)(2,1)S(1)}, u32[]{:S(2)}, u32[]{:S(2)}) collective-permute-start(bf16[2,66,256]{2,1,0:T(8,128)(2,1)S(1)} %slice.1035), channel_id=1, source_target_pairs={{0,4},{4,8},{8,12},{12,0},{1,5},{5,9},{9,13},{13,1},{2,6},{6,10},{... | collective-permute-start | bytes 202760 | tf_op jit(solution)/shard_map/ppermute | solution.py:20
  64.7 6.9 %collective-permute-start.9 = (bf16[2,66,256]{2,1,0:T(8,128)(2,1)S(1)}, bf16[2,66,256]{2,1,0:T(8,128)(2,1)S(1)}, u32[]{:S(2)}, u32[]{:S(2)}) collective-permute-start(bf16[2,66,256]{2,1,0:T(8,128)(2,1)S(1)} %slice.1035), channel_id=1, source_target_pairs={{0,12},{4,0},{8,4},{12,8},{1,13},{5,1},{9,5},{13,9},{2,14},{6,2},{... | collective-permute-start | bytes 202760 | tf_op jit(solution)/shard_map/ppermute | solution.py:20
  72.3 5.0 %collective-permute-start.11 = (bf16[2,64,256]{2,1,0:T(8,128)(2,1)S(1)}, bf16[2,64,256]{2,1,0:T(8,128)(2,1)S(1)}, u32[]{:S(2)}, u32[]{:S(2)}) collective-permute-start(bf16[2,64,256]{2,1,0:T(8,128)(2,1)S(1)} %fusion.66), channel_id=1, source_target_pairs={{0,12},{4,0},{8,4},{12,8},{1,13},{5,1},{9,5},{13,9},{2,14},{6,2},{... | collective-permute-start | bytes 196616 | tf_op jit(solution)/shard_map/ppermute | solution.py:20
  75.4 6.1 %collective-permute-start.12 = (bf16[2,64,256]{2,1,0:T(8,128)(2,1)S(1)}, bf16[2,64,256]{2,1,0:T(8,128)(2,1)S(1)}, u32[]{:S(2)}, u32[]{:S(2)}) collective-permute-start(bf16[2,64,256]{2,1,0:T(8,128)(2,1)S(1)} %fusion.66), channel_id=1, source_target_pairs={{0,4},{4,8},{8,12},{12,0},{1,5},{5,9},{9,13},{13,1},{2,6},{6,10},{... | collective-permute-start | bytes 196616 | tf_op jit(solution)/shard_map/ppermute | solution.py:20

commit v4 on v3

--- a/solution.py
+++ b/solution.py
@@ -242,22 +242,36 @@
     return value[..., rows : value.shape[-2] - rows, :]
 
 
-def force(up, down, here, below, forward, ahead, prior, backward):
-    pulls = here * (spring(up - forward) - spring(-up - ahead))
-    return step_size * (pulls + below * (spring(down - backward) - spring(-down - prior)))
-
-
-def prefix(pair_sum, section):
+def pair_part(apart, here, forward, ahead):
+    return step_size * here * (spring(apart - forward) - spring(-apart - ahead))
+
+
+def split(value):
+    high = lax.reduce_precision(value, 8, 7)
+    return [high.astype(jnp.bfloat16), (value - high).astype(jnp.bfloat16)]
+
+
+def joined(parts):
+    return parts[:2].astype(jnp.float32) + parts[2:4].astype(jnp.float32)
+
+
+def running(gain, section):
     count = lax.axis_size("gz")
-
-    def earlier(value, steps):
-        return jnp.where(section >= steps, ringed(value, "gz", steps), 0.0)
-
-    reach = 2
-    while reach < count - 2:
-        pair_sum = pair_sum + earlier(pair_sum, reach)
-        reach *= 2
-    return earlier(pair_sum, 2)
+    reach = 1
+    while count > 4 and reach < count - 2:
+        more = jnp.where(section >= reach, ringed(gain, "gz", reach), 0.0)
+        gain, reach = gain + more, 2 * reach
+    return gain
+
+
+def messages(flow, here, section):
+    forward, ahead = flow[:2], flow[2:]
+    gain = here * (forward - ahead)
+    part = pair_part(0.5 * gain, here, forward, ahead).astype(jnp.bfloat16)
+    halves = split(gain)
+    to_next = jnp.concatenate([*halves, forward.astype(jnp.bfloat16)])
+    to_second = jnp.concatenate([*split(running(gain, section)), part])
+    return to_next, to_second, jnp.concatenate([part, *halves])
 
 
 def on_device(features, class_map, stiffness, valid):
@@ -298,45 +312,6 @@
         if low <= row < high:
             return 0, row - low
         return (1, row + RADIUS) if row < low else (1, row - high + outer)
-
-    live = jnp.where(section < sections - 1, 1.0, 0.0)[None]
-    middle_rows = range(quarter, height - quarter, BLOCK)
-    middle = flows(live, [center], [upper_mid], own_at, upper_at, middle_rows)
-    lower_mid = ringed(
-        jnp.concatenate([middle.reshape(-1, breadth), own_codes.astype(jnp.float32)]), "gz", 1
-    )
-    outer_rows = [*range(0, quarter, BLOCK), *range(height - quarter, height, BLOCK)]
-    outside = flows(
-        live, [center, before, after], [upper_mid, upper_out], own_at, upper_at, outer_rows
-    )
-
-    head, tail = outside[:, :quarter], outside[:, quarter:]
-    head = jnp.concatenate([ringed(tail[:, -STEPS:], tile_axes, 1), head], axis=1)
-    tail = jnp.concatenate([tail, ringed(outside[:, :STEPS], tile_axes, -1)], axis=1)
-    lower_out = ringed(jnp.concatenate([head, tail], axis=1), "gz", 1)
-    both = jnp.concatenate([head, middle, tail], axis=1)
-    n_mid = middle.shape[0] * middle.shape[1]
-    lower = jnp.concatenate(
-        [
-            lower_out[:, : head.shape[1]],
-            lower_mid[:n_mid].reshape(middle.shape),
-            lower_out[:, head.shape[1] :],
-        ],
-        axis=1,
-    )
-    fwd, ahd = both[:2], both[2:]
-    pri, bwd = lower[:2], lower[2:]
-    forward = fwd[:, STEPS:-STEPS]
-
-    def stiff_of(code):
-        levels = jnp.arange(stiffness.shape[0], dtype=jnp.float32)[:, None, None] + 1.0
-        code = code.astype(jnp.float32)
-        field = jnp.sum(jnp.where(code[None] == levels, stiffness[:, None, None], 0.0), axis=0)
-        return field, code > 0.0
-
-    stiff, inside = stiff_of(own_codes)
-    stiff_up, inside_up = stiff_of(upper_codes)
-    stiff_down, inside_down = stiff_of(lower_mid[n_mid:])
 
     sound = jnp.pad(valid.astype(jnp.float32), ((1, 1), (1, 1)))
     near = lax.dynamic_slice(sound, (section, tile), (3, 3))
@@ -348,37 +323,92 @@
         ],
         axis=1,
     )
+
+    def own_links(begin, count):
+        return by_row[1][None, begin : begin + count, None]
+
+    live = jnp.where(section < sections - 1, 1.0, 0.0)[None]
+    middle_rows = range(quarter, height - quarter, BLOCK)
+    middle = flows(live, [center], [upper_mid], own_at, upper_at, middle_rows)
+    by_mid = own_links(quarter + STEPS, height // 2)
+    sent_mid = messages(middle, by_mid, section)
+    n_mid = 6 * middle.shape[1]
+    below_mid = ringed(jnp.concatenate([sent_mid[0].reshape(n_mid, breadth), own_codes]), "gz", 1)
+    before_mid = ringed(sent_mid[1], "gz", 2)
+    above_mid = ringed(sent_mid[2], "gz", -1)
+    outer_rows = [*range(0, quarter, BLOCK), *range(height - quarter, height, BLOCK)]
+    outside = flows(
+        live, [center, before, after], [upper_mid, upper_out], own_at, upper_at, outer_rows
+    )
+
+    head, tail = outside[:, :quarter], outside[:, quarter:]
+    head = jnp.concatenate([ringed(tail[:, -STEPS:], tile_axes, 1), head], axis=1)
+    tail = jnp.concatenate([tail, ringed(outside[:, :STEPS], tile_axes, -1)], axis=1)
+    edge_rows = jnp.concatenate([head, tail], axis=1)
+    first_tail = head.shape[1]
+    by_edge = jnp.concatenate(
+        [own_links(0, first_tail), own_links(height + 2 * STEPS - first_tail, first_tail)], axis=1
+    )
+    sent_out = messages(edge_rows, by_edge, section)
+    below_out = ringed(sent_out[0], "gz", 1)
+    before_out = ringed(sent_out[1], "gz", 2)
+    above_out = ringed(sent_out[2], "gz", -1)
+
+    def whole(inner, outer):
+        return jnp.concatenate([outer[:, :first_tail], inner, outer[:, first_tail:]], axis=1)
+
+    both = whole(middle, edge_rows)
+    fwd, ahd = both[:2], both[2:]
+    from_below = whole(below_mid[:n_mid].reshape(6, -1, breadth), below_out)
+    from_before = whole(before_mid, before_out)
+    from_above = whole(above_mid, above_out)
+    gain_below, pri = joined(from_below), from_below[4:].astype(jnp.float32)
+    bwd = pri - gain_below
+    part_before = from_before[4:].astype(jnp.float32)
+    part_above = from_above[:2].astype(jnp.float32)
+    earlier = jnp.where(section > 1, joined(from_before), 0.0)
+    if sections <= 4:
+        earlier = earlier + jnp.where(section > 2, joined(from_above[2:]), 0.0)
+    forward = fwd[:, STEPS:-STEPS]
+
+    def stiff_of(code):
+        levels = jnp.arange(stiffness.shape[0], dtype=jnp.float32)[:, None, None] + 1.0
+        code = code.astype(jnp.float32)
+        field = jnp.sum(jnp.where(code[None] == levels, stiffness[:, None, None], 0.0), axis=0)
+        return field, code > 0.0
+
+    stiff, inside = stiff_of(own_codes)
+    stiff_up, inside_up = stiff_of(upper_codes)
+    stiff_down, inside_down = stiff_of(below_mid[n_mid:])
+
     below, here = by_row[0][None, :, None], by_row[1][None, :, None]
 
     gain = here * (fwd - ahd)
-    gain_below = below * (pri - bwd)
-    start = 0.5 * (prefix(gain + gain_below, section) + gain_below)
-    pull = force(0.5 * gain, -0.5 * gain_below, here, below, fwd, ahd, pri, bwd)
-    sent = trim(2, pull).astype(jnp.bfloat16)
-    pull_up = ringed(sent, "gz", -1).astype(jnp.float32)
-    pull_down = ringed(sent, "gz", 1).astype(jnp.float32)
+    start = 0.5 * (earlier + gain_below)
+    part = pair_part(0.5 * gain, here, fwd, ahd)
+    part_below = pair_part(0.5 * gain_below, below, pri, bwd)
 
     start_up = start + 0.5 * gain
     start_down = start - 0.5 * gain_below
-    first = relaxed(start, stiff, inside) + trim(1, pull)
-    first_up = relaxed(trim(1, start_up), trim(1, stiff_up), trim(1, inside_up)) + pull_up
-    first_down = (
-        relaxed(trim(1, start_down), trim(1, stiff_down), trim(1, inside_down)) + pull_down
-    )
+    first = relaxed(start, stiff, inside) + trim(1, part - part_below)
+    first_up = relaxed(trim(1, start_up), trim(1, stiff_up), trim(1, inside_up)) + trim(
+        2, part_above - part
+    )
+    first_down = relaxed(
+        trim(1, start_down), trim(1, stiff_down), trim(1, inside_down)
+    ) + trim(2, part_below - part_before)
     mid = trim(1, first)
-    fields = [trim(2, x) for x in (here, below, fwd, ahd, pri, bwd)]
-    second = relaxed(first, trim(1, stiff), trim(1, inside)) + force(
-        first_up - mid, first_down - mid, *fields
-    )
-    change = trim(1, second) - trim(3, start)
-    change = change.astype(jnp.bfloat16)
+    up = [trim(2, x) for x in (here, fwd, ahd)]
+    down = [trim(2, x) for x in (below, pri, bwd)]
+    second = relaxed(first, trim(1, stiff), trim(1, inside))
+    second = second + pair_part(first_up - mid, *up) - pair_part(mid - first_down, *down)
+    change = (trim(1, second) - trim(3, start)).astype(jnp.bfloat16)
     last_up = trim(3, start_up) + ringed(change, "gz", -1).astype(jnp.float32)
     last_down = trim(3, start_down) + ringed(change, "gz", 1).astype(jnp.float32)
-    fields = [trim(1, x) for x in fields]
     mid = trim(1, second)
-    third = relaxed(second, trim(2, stiff), trim(2, inside)) + force(
-        last_up - mid, last_down - mid, *fields
-    )
+    up, down = ([trim(1, x) for x in fields] for fields in (up, down))
+    third = relaxed(second, trim(2, stiff), trim(2, inside))
+    third = third + pair_part(last_up - mid, *up) - pair_part(mid - last_down, *down)
     return (third[None], forward[None])
 
 

time: 83.4 us -> 82.7 us (level)
  waiting for transfers between devices: 29.4 us -> 23 us
  local copies, waits for them, and re-layouts: 4.05 us -> 6.72 us
  other arithmetic: 4.79 us -> 6.39 us
    ppermute x13 -> x14, waiting for transfers between devices: 29.4 us -> 23 us  [ringed(): lax.ppermute(value, axis, [(i, (i + steps) % count) for i in range(count)])]
    slice x3 -> x11, local copies, waits for them, and re-layouts: 0.03 us -> 2.23 us  [the longest x2 0.86 us: on_device(): part_above = from_above[:2].astype(jnp.float32)]
    reduce_sum x5 -> x7, other arithmetic: 1.43 us -> 2.12 us  [spring(): squares = jnp.sum(vector * vector, axis=0, keepdims=True)]
    unnamed x11 -> x15, local copies, waits for them, and re-layouts: 2.7 us -> 3.26 us
    ppermute x13 -> x14, starting transfers between devices: 21.3 us -> 21.8 us  [ringed(): lax.ppermute(value, axis, [(i, (i + steps) % count) for i in range(count)])]
  transfers between devices with their start and end apart: 13 -> 14, of which waited for: 7 -> 6; matrix products, arithmetic and copies ran while one was open for 3% -> 5% of each run, Pallas kernels for 27% -> 27%
where the time goes in v4:
time: 82.7 us; the launch traced here: 82.4 us
  waiting for transfers between devices  23 us (28%)
  Pallas kernels  22.5 us (27%)
  starting transfers between devices  21.8 us (26%)
  local copies, waits for them, and re-layouts  6.72 us (8%)
  other arithmetic  6.39 us (8%)
  between operations  1.98 us (2%)
    ppermute x14, waiting for transfers between devices, ringed(): lax.ppermute(value, axis, [(i, (i + steps) % count) for i in range(count)])  23 us
    pallas_call x2, Pallas kernels, flows(): pl.pallas_call(functools.partial(flow_kernel, *tables, len(early)), out_s...  22.5 us
    ppermute x14, starting transfers between devices, ringed(): lax.ppermute(value, axis, [(i, (i + steps) % count) for i in range(count)])  21.8 us
    unnamed x15, local copies, waits for them, and re-layouts  3.26 us
    reduce_sum x7, other arithmetic, spring(): squares = jnp.sum(vector * vector, axis=0, keepdims=True)  2.12 us
  transfers between devices with their start and end apart: 14, of which 6 were waited for; matrix products, arithmetic and copies ran while one was open for 5% of the time, Pallas kernels for 27%

profile of v4, /device:TPU:0, one launch (start us, length us, event | category | flops | bytes accessed | tf_op | source)
XLA Modules:
  0.0 82.4 jit_solution(11868353296019051151)
XLA Ops:
  0.6 1.4 %copy.9 = bf16[1,16,64,256]{3,1,2,0:T(8,128)(2,1)S(1)} copy(bf16[1,16,64,256]{3,2,1,0:T(8,128)(2,1)} %param.4) | data formatting | bytes 1048576 | tf_op args[0]
  2.6 2.0 %collective-permute-start.1 = (bf16[7,16,256]{2,1,0:T(8,128)(2,1)S(1)}, bf16[7,16,256]{2,1,0:T(8,128)(2,1)S(1)}, u32[]{:S(2)}, u32[]{:S(2)}) collective-permute-start(bf16[7,16,256]{2,1,0:T(8,128)(2,1)S(1)} %pad_maximum_fusion.15), channel_id=1, source_target_pairs={{0,3},{1,0},{2,1},{3,2},{4,7},{5,4},{6,5},{7,6},{8,11},{9,8},{10,9... | collective-permute-start | bytes 172040 | tf_op jit(solution)/shard_map/ppermute | solution.py:20
  4.6 4.4 %collective-permute-start.2 = (bf16[44,16,256]{2,1,0:T(8,128)(2,1)S(1)}, bf16[44,16,256]{2,1,0:T(8,128)(2,1)S(1)}, u32[]{:S(2)}, u32[]{:S(2)}) collective-permute-start(bf16[44,16,256]{2,1,0:T(8,128)(2,1)S(1)} %slice.600), channel_id=1, source_target_pairs={{0,12},{4,0},{8,4},{12,8},{1,13},{5,1},{9,5},{13,9},{2,14},{6,2},{... | collective-permute-start | bytes 1081352 | tf_op jit(solution)/shard_map/ppermute | solution.py:20
  9.1 0.7 copy-done.3
  12.9 5.0 %collective-permute-done.2.refs_3_.refs_1_ = bf16[44,16,256]{2,1,0:T(8,128)(2,1)S(1)} collective-permute-done((bf16[44,16,256]{2,1,0:T(8,128)(2,1)S(1)}, bf16[44,16,256]{2,1,0:T(8,128)(2,1)S(1)}, u32[]{:S(2)}, u32[]{:S(2)}) %collective-permute-start.2) | collective-permute-done | bytes 360480 | tf_op jit(solution)/shard_map/ppermute | solution.py:20
  17.9 11.3 %flows.3 = f32[4,32,256]{2,1,0:T(8,128)S(1)} custom-call(f32[1]{0:T(128)} %bitcast.9.live_ref, bf16[64,16,256]{2,1,0:T(8,128)(2,1)S(1)} %bitcast.149, bf16[44,16,256]{2,1,0:T(8,128)(2,1)S(1)} %collective-permute-done.2.refs_3_.refs_1_), custom_call_target="tpu_custom_call" | custom-call | flops 2147483648 | bytes 4194304 | tf_op jit(solution)/shard_map/flows/pallas_call | solution.py:200
  29.2 0.7 multiply_reduce_fusion.15
  30.5 3.9 %collective-permute-start.9 = (bf16[6,32,256]{2,1,0:T(8,128)(2,1)S(1)}, bf16[6,32,256]{2,1,0:T(8,128)(2,1)S(1)}, u32[]{:S(2)}, u32[]{:S(2)}) collective-permute-start(bf16[6,32,256]{2,1,0:T(8,128)(2,1)S(1)} %get-tuple-element.74), channel_id=1, source_target_pairs={{0,12},{4,0},{8,4},{12,8},{1,13},{5,1},{9,5},{13,9},{2,14},{6,2},{... | collective-permute-start | bytes 294920 | tf_op jit(solution)/shard_map/ppermute | solution.py:20
  34.9 11.3 %flows.2 = f32[4,32,256]{2,1,0:T(8,128)S(1)} custom-call(f32[1]{0:T(128)} %bitcast.9.live_ref, bf16[64,16,256]{2,1,0:T(8,128)(2,1)S(1)} %bitcast.150, bf16[7,16,256]{2,1,0:T(8,128)(2,1)S(1)} %broadcast_select_fusion.1.refs_1_, bf16[7,16,256]{2,1,0:T(8,128)(2,1)S(1)} %broadcast_select_fusion.refs_2_, ...), custom_call_target="tpu_custom_call" | custom-call | flops 2147483648 | bytes 4194304 | tf_op jit(solution)/shard_map/flows/pallas_call | solution.py:200
  46.3 1.7 %collective-permute-start.5 = (f32[4,3,256]{2,1,0:T(4,128)S(1)}, f32[4,3,256]{2,1,0:T(4,128)S(1)}, u32[]{:S(2)}, u32[]{:S(2)}) collective-permute-start(f32[4,3,256]{2,1,0:T(4,128)S(1)} %get-tuple-element.61), channel_id=1, source_target_pairs={{0,3},{1,0},{2,1},{3,2},{4,7},{5,4},{6,5},{7,6},{8,11},{9,8},{10,9... | collective-permute-start | bytes 36872 | tf_op jit(solution)/shard_map/ppermute | solution.py:20
  48.0 1.4 %collective-permute-done.4 = f32[4,3,256]{2,1,0:T(4,128)S(1)} collective-permute-done((f32[4,3,256]{2,1,0:T(4,128)S(1)}, f32[4,3,256]{2,1,0:T(4,128)S(1)}, u32[]{:S(2)}, u32[]{:S(2)}) %collective-permute-start.4) | collective-permute-done | bytes 12320 | tf_op jit(solution)/shard_map/ppermute | solution.py:20
  49.7 1.5 %collective-permute-start.8 = (bf16[6,38,256]{2,1,0:T(8,128)(2,1)S(1)}, bf16[6,38,256]{2,1,0:T(8,128)(2,1)S(1)}, u32[]{:S(2)}, u32[]{:S(2)}) collective-permute-start(bf16[6,38,256]{2,1,0:T(8,128)(2,1)S(1)} %get-tuple-element.68), channel_id=1, source_target_pairs={{0,12},{4,0},{8,4},{12,8},{1,13},{5,1},{9,5},{13,9},{2,14},{6,2},{... | collective-permute-start | bytes 350216 | tf_op jit(solution)/shard_map/ppermute | solution.py:20
  52.4 2.7 %collective-permute-done.8 = bf16[6,38,256]{2,1,0:T(8,128)(2,1)S(1)} collective-permute-done((bf16[6,38,256]{2,1,0:T(8,128)(2,1)S(1)}, bf16[6,38,256]{2,1,0:T(8,128)(2,1)S(1)}, u32[]{:S(2)}, u32[]{:S(2)}) %collective-permute-start.8) | collective-permute-done | bytes 116768 | tf_op jit(solution)/shard_map/ppermute | solution.py:20
  55.1 2.7 %collective-permute-start.6 = (bf16[6,38,256]{2,1,0:T(8,128)(2,1)S(1)}, bf16[6,38,256]{2,1,0:T(8,128)(2,1)S(1)}, u32[]{:S(2)}, u32[]{:S(2)}) collective-permute-start(bf16[6,38,256]{2,1,0:T(8,128)(2,1)S(1)} %get-tuple-element.67), channel_id=1, source_target_pairs={{0,8},{4,12},{8,0},{12,4},{1,9},{5,13},{9,1},{13,5},{2,10},{6,14},... | collective-permute-start | bytes 350216 | tf_op jit(solution)/shard_map/ppermute | solution.py:20
  57.8 7.9 %collective-permute-done.6 = bf16[6,38,256]{2,1,0:T(8,128)(2,1)S(1)} collective-permute-done((bf16[6,38,256]{2,1,0:T(8,128)(2,1)S(1)}, bf16[6,38,256]{2,1,0:T(8,128)(2,1)S(1)}, u32[]{:S(2)}, u32[]{:S(2)}) %collective-permute-start.6) | collective-permute-done | bytes 116768 | tf_op jit(solution)/shard_map/ppermute | solution.py:20
  67.0 0.6 copy-done.4
  67.7 0.7 select_reduce_fusion.1
  69.0 0.7 slice-done
  70.2 0.9 %slice-done.1 = bf16[2,70,256]{2,1,0:T(8,128)(2,1)S(1)} async-done(((bf16[6,70,256]{2,1,0:T(8,128)(2,1)}), bf16[2,70,256]{2,1,0:T(8,128)(2,1)S(1)}, s32[]{:S(2)}) %slice-start.1) | async-done | bytes 71704 | tf_op jit(solution)/shard_map/slice | solution.py:368
  71.8 2.8 %collective-permute-start.12 = (bf16[2,64,256]{2,1,0:T(8,128)(2,1)S(1)}, bf16[2,64,256]{2,1,0:T(8,128)(2,1)S(1)}, u32[]{:S(2)}, u32[]{:S(2)}) collective-permute-start(bf16[2,64,256]{2,1,0:T(8,128)(2,1)S(1)} %fusion.68), channel_id=1, source_target_pairs={{0,12},{4,0},{8,4},{12,8},{1,13},{5,1},{9,5},{13,9},{2,14},{6,2},{... | collective-permute-start | bytes 196616 | tf_op jit(solution)/shard_map/ppermute | solution.py:20
  74.7 2.2 %collective-permute-done.12 = bf16[2,64,256]{2,1,0:T(8,128)(2,1)S(1)} collective-permute-done((bf16[2,64,256]{2,1,0:T(8,128)(2,1)S(1)}, bf16[2,64,256]{2,1,0:T(8,128)(2,1)S(1)}, u32[]{:S(2)}, u32[]{:S(2)}) %collective-permute-start.12) | collective-permute-done | bytes 65568 | tf_op jit(solution)/shard_map/ppermute | solution.py:20
  76.8 3.8 %collective-permute-done.13 = bf16[2,64,256]{2,1,0:T(8,128)(2,1)S(1)} collective-permute-done((bf16[2,64,256]{2,1,0:T(8,128)(2,1)S(1)}, bf16[2,64,256]{2,1,0:T(8,128)(2,1)S(1)}, u32[]{:S(2)}, u32[]{:S(2)}) %collective-permute-start.13) | collective-permute-done | bytes 65568 | tf_op jit(solution)/shard_map/ppermute | solution.py:20
  80.6 0.8 multiply_reduce_fusion.11
  81.5 0.9 %fusion.64 = f32[1,2,64,256]{3,2,1,0:T(8,128)} fusion(f32[2,66,256]{2,1,0:T(8,128)S(1)} %fusion.18, f32[64,256]{1,0:T(8,128)S(1)} %add_sqrt_fusion.8, f32[64,256]{1,0:T(8,128)S(1)} %add_sqrt_fusion.9, f32[64]{0:T(128)S(1)} %get-tuple-element.97, f32[64,256]{1,0:T(8,128)S(1)} %add_sqrt_fusion.10, f32[64,256]{1,0:T(8,128)S(1)} %add_sqrt_fusion.11, ...), kind=kLoop, calls=%fused_computation.115 | loop fusion | flops 983040 | bytes 1999872 | tf_op jit(solution)/shard_map/broadcast_in_dim | solution.py:412
  (127 shorter events, 8.7 us)
Async XLA Ops:
  0.6 1.4 %copy-start.2 = (s32[1,64,256]{2,1,0:T(8,128)S(1)}, s32[1,64,256]{2,1,0:T(8,128)}, u32[]{:S(2)}) copy-start(s32[1,64,256]{2,1,0:T(8,128)} %param.5) | copy-start | bytes 196612
  2.1 10.0 %collective-permute-start = (bf16[7,16,256]{2,1,0:T(8,128)(2,1)S(1)}, bf16[7,16,256]{2,1,0:T(8,128)(2,1)S(1)}, u32[]{:S(2)}, u32[]{:S(2)}) collective-permute-start(bf16[7,16,256]{2,1,0:T(8,128)(2,1)S(1)} %pad_maximum_fusion.14), channel_id=1, source_target_pairs={{0,1},{1,2},{2,3},{3,0},{4,5},{5,6},{6,7},{7,4},{8,9},{9,10},{10,1... | collective-permute-start | bytes 172040 | tf_op jit(solution)/shard_map/ppermute | solution.py:20
  2.6 9.5 %collective-permute-start.1 = (bf16[7,16,256]{2,1,0:T(8,128)(2,1)S(1)}, bf16[7,16,256]{2,1,0:T(8,128)(2,1)S(1)}, u32[]{:S(2)}, u32[]{:S(2)}) collective-permute-start(bf16[7,16,256]{2,1,0:T(8,128)(2,1)S(1)} %pad_maximum_fusion.15), channel_id=1, source_target_pairs={{0,3},{1,0},{2,1},{3,2},{4,7},{5,4},{6,5},{7,6},{8,11},{9,8},{10,9... | collective-permute-start | bytes 172040 | tf_op jit(solution)/shard_map/ppermute | solution.py:20
  4.6 13.2 %collective-permute-start.2 = (bf16[44,16,256]{2,1,0:T(8,128)(2,1)S(1)}, bf16[44,16,256]{2,1,0:T(8,128)(2,1)S(1)}, u32[]{:S(2)}, u32[]{:S(2)}) collective-permute-start(bf16[44,16,256]{2,1,0:T(8,128)(2,1)S(1)} %slice.600), channel_id=1, source_target_pairs={{0,12},{4,0},{8,4},{12,8},{1,13},{5,1},{9,5},{13,9},{2,14},{6,2},{... | collective-permute-start | bytes 1081352 | tf_op jit(solution)/shard_map/ppermute | solution.py:20
  9.1 0.7 copy-start.3
  12.4 22.5 %collective-permute-start.3 = (bf16[37,16,256]{2,1,0:T(8,128)(2,1)S(1)}, bf16[37,16,256]{2,1,0:T(8,128)(2,1)S(1)}, u32[]{:S(2)}, u32[]{:S(2)}) collective-permute-start(bf16[37,16,256]{2,1,0:T(8,128)(2,1)S(1)} %constant_dynamic-update-slice_fusion), channel_id=1, source_target_pairs={{0,12},{4,0},{8,4},{12,8},{1,13},{5,1},{9,5},{13,9},{2,14},{6,2},{... | collective-permute-start | bytes 909320 | tf_op jit(solution)/shard_map/ppermute | solution.py:20
  30.0 36.0 %collective-permute-start.11 = (bf16[262,256]{1,0:T(8,128)(2,1)S(1)}, bf16[262,256]{1,0:T(8,128)(2,1)S(1)}, u32[]{:S(2)}, u32[]{:S(2)}) collective-permute-start(bf16[262,256]{1,0:T(8,128)(2,1)S(1)} %pad_maximum_fusion.5), channel_id=1, source_target_pairs={{0,4},{4,8},{8,12},{12,0},{1,5},{5,9},{9,13},{13,1},{2,6},{6,10},{... | collective-permute-start | bytes 402440 | tf_op jit(solution)/shard_map/ppermute | solution.py:20
  30.5 35.3 %collective-permute-start.9 = (bf16[6,32,256]{2,1,0:T(8,128)(2,1)S(1)}, bf16[6,32,256]{2,1,0:T(8,128)(2,1)S(1)}, u32[]{:S(2)}, u32[]{:S(2)}) collective-permute-start(bf16[6,32,256]{2,1,0:T(8,128)(2,1)S(1)} %get-tuple-element.74), channel_id=1, source_target_pairs={{0,12},{4,0},{8,4},{12,8},{1,13},{5,1},{9,5},{13,9},{2,14},{6,2},{... | collective-permute-start | bytes 294920 | tf_op jit(solution)/shard_map/ppermute | solution.py:20
  34.4 31.4 %collective-permute-start.7 = (bf16[6,32,256]{2,1,0:T(8,128)(2,1)S(1)}, bf16[6,32,256]{2,1,0:T(8,128)(2,1)S(1)}, u32[]{:S(2)}, u32[]{:S(2)}) collective-permute-start(bf16[6,32,256]{2,1,0:T(8,128)(2,1)S(1)} %get-tuple-element.73), channel_id=1, source_target_pairs={{0,8},{4,12},{8,0},{12,4},{1,9},{5,13},{9,1},{13,5},{2,10},{6,14},... | collective-permute-start | bytes 294920 | tf_op jit(solution)/shard_map/ppermute | solution.py:20
  46.2 3.2 %collective-permute-start.4 = (f32[4,3,256]{2,1,0:T(4,128)S(1)}, f32[4,3,256]{2,1,0:T(4,128)S(1)}, u32[]{:S(2)}, u32[]{:S(2)}) collective-permute-start(f32[4,3,256]{2,1,0:T(4,128)S(1)} %get-tuple-element.62), channel_id=1, source_target_pairs={{0,1},{1,2},{2,3},{3,0},{4,5},{5,6},{6,7},{7,4},{8,9},{9,10},{10,1... | collective-permute-start | bytes 36872 | tf_op jit(solution)/shard_map/ppermute | solution.py:20
  46.3 3.2 %collective-permute-start.5 = (f32[4,3,256]{2,1,0:T(4,128)S(1)}, f32[4,3,256]{2,1,0:T(4,128)S(1)}, u32[]{:S(2)}, u32[]{:S(2)}) collective-permute-start(f32[4,3,256]{2,1,0:T(4,128)S(1)} %get-tuple-element.61), channel_id=1, source_target_pairs={{0,3},{1,0},{2,1},{3,2},{4,7},{5,4},{6,5},{7,6},{8,11},{9,8},{10,9... | collective-permute-start | bytes 36872 | tf_op jit(solution)/shard_map/ppermute | solution.py:20
  49.7 5.4 %collective-permute-start.8 = (bf16[6,38,256]{2,1,0:T(8,128)(2,1)S(1)}, bf16[6,38,256]{2,1,0:T(8,128)(2,1)S(1)}, u32[]{:S(2)}, u32[]{:S(2)}) collective-permute-start(bf16[6,38,256]{2,1,0:T(8,128)(2,1)S(1)} %get-tuple-element.68), channel_id=1, source_target_pairs={{0,12},{4,0},{8,4},{12,8},{1,13},{5,1},{9,5},{13,9},{2,14},{6,2},{... | collective-permute-start | bytes 350216 | tf_op jit(solution)/shard_map/ppermute | solution.py:20
  51.3 14.6 %collective-permute-start.10 = (bf16[6,38,256]{2,1,0:T(8,128)(2,1)S(1)}, bf16[6,38,256]{2,1,0:T(8,128)(2,1)S(1)}, u32[]{:S(2)}, u32[]{:S(2)}) collective-permute-start(bf16[6,38,256]{2,1,0:T(8,128)(2,1)S(1)} %get-tuple-element.75), channel_id=1, source_target_pairs={{0,4},{4,8},{8,12},{12,0},{1,5},{5,9},{9,13},{13,1},{2,6},{6,10},{... | collective-permute-start | bytes 350216 | tf_op jit(solution)/shard_map/ppermute | solution.py:20
  55.1 10.6 %collective-permute-start.6 = (bf16[6,38,256]{2,1,0:T(8,128)(2,1)S(1)}, bf16[6,38,256]{2,1,0:T(8,128)(2,1)S(1)}, u32[]{:S(2)}, u32[]{:S(2)}) collective-permute-start(bf16[6,38,256]{2,1,0:T(8,128)(2,1)S(1)} %get-tuple-element.67), channel_id=1, source_target_pairs={{0,8},{4,12},{8,0},{12,4},{1,9},{5,13},{9,1},{13,5},{2,10},{6,14},... | collective-permute-start | bytes 350216 | tf_op jit(solution)/shard_map/ppermute | solution.py:20
  65.8 0.7 copy-start
  65.9 0.7 copy-start.1
  67.0 0.7 copy-start.4
  68.8 0.9 %slice-start = ((bf16[6,70,256]{2,1,0:T(8,128)(2,1)}), bf16[2,70,256]{2,1,0:T(8,128)(2,1)S(1)}, s32[]{:S(2)}) async-start(bf16[6,70,256]{2,1,0:T(8,128)(2,1)} %copy-done), calls=%async_computation | async-start | bytes 147456 | tf_op jit(solution)/shard_map/slice | solution.py:367
  70.1 0.9 %slice-start.1 = ((bf16[6,70,256]{2,1,0:T(8,128)(2,1)}), bf16[2,70,256]{2,1,0:T(8,128)(2,1)S(1)}, s32[]{:S(2)}) async-start(bf16[6,70,256]{2,1,0:T(8,128)(2,1)} %copy-done.1), calls=%async_computation.1 | async-start | bytes 147456 | tf_op jit(solution)/shard_map/slice | solution.py:368
  71.8 5.1 %collective-permute-start.12 = (bf16[2,64,256]{2,1,0:T(8,128)(2,1)S(1)}, bf16[2,64,256]{2,1,0:T(8,128)(2,1)S(1)}, u32[]{:S(2)}, u32[]{:S(2)}) collective-permute-start(bf16[2,64,256]{2,1,0:T(8,128)(2,1)S(1)} %fusion.68), channel_id=1, source_target_pairs={{0,12},{4,0},{8,4},{12,8},{1,13},{5,1},{9,5},{13,9},{2,14},{6,2},{... | collective-permute-start | bytes 196616 | tf_op jit(solution)/shard_map/ppermute | solution.py:20
  74.5 6.1 %collective-permute-start.13 = (bf16[2,64,256]{2,1,0:T(8,128)(2,1)S(1)}, bf16[2,64,256]{2,1,0:T(8,128)(2,1)S(1)}, u32[]{:S(2)}, u32[]{:S(2)}) collective-permute-start(bf16[2,64,256]{2,1,0:T(8,128)(2,1)S(1)} %fusion.68), channel_id=1, source_target_pairs={{0,4},{4,8},{8,12},{12,0},{1,5},{5,9},{9,13},{13,1},{2,6},{6,10},{... | collective-permute-start | bytes 196616 | tf_op jit(solution)/shard_map/ppermute | solution.py:20
